TPU v7x, 256 devices: a whole 4x4x8 slice. The times are simulated.
256 devices in a mesh: req: 8 (over y_hi, x), blk: 32 (over y_lo, z, core).
Axes of the slice: x: 4, y: 4 (y_hi: 2, y_lo: 2; y = y_hi * 2 + y_lo), z: 8, core: 2. Of those that a mesh axis runs over, the one named last changes fastest.
Arguments:
- prefill_resid: bfloat16 [1024, 2048], P(('blk', 'req')), may hold values from -3 to 3
- prefill_routes: int32 [1024, 6], P(('blk', 'req')), may hold values from 0 to 63, all different within a row; in each aligned block of 32 rows (0 to 31, 32 to 63, ...) at most 6 rows name the same one
- prefill_scores: float32 [1024, 6], P(('blk', 'req')), may hold values from 0.05 to 1
- decode_resid: bfloat16 [16, 2048], P('req'), may hold values from -3 to 3
- queries: bfloat16 [16, 16, 192], P('req'), may hold values from -8 to 8
- latent_cache: bfloat16 [16, 16384, 576], P('req', 'blk'), may hold values from -8 to 8
- new_latent: bfloat16 [16, 576], P('req'), may hold values from -8 to 8
- cache_lengths: int32 [16], P('req'), may hold values from 1 to 16384, 65536 in all
- decode_routes: int32 [16, 6], P('req'), may hold values from 0 to 63, all different within a row
- decode_scores: float32 [16, 6], P('req'), may hold values from 0.05 to 1
- norm_gain: float32 [2048], replicated, may hold values from 0.1 to 1.9
- absorb_key: bfloat16 [16, 128, 512], replicated, may hold values from -0.5 to 0.5
- absorb_value: bfloat16 [16, 512, 128], P('req'), may hold values from -6 to 6
- out_proj: bfloat16 [16, 128, 2048], P('req'), may hold values from -0.125 to 0.125
- expert_gate: bfloat16 [64, 2048, 1408], P('blk', None, 'req'), may hold values from -0.125 to 0.125
- expert_up: bfloat16 [64, 2048, 1408], P('blk', None, 'req'), may hold values from -0.125 to 0.125
- expert_down: bfloat16 [64, 1408, 2048], P('blk', 'req'), may hold values from -0.15625 to 0.15625
- shared_gate: bfloat16 [2048, 2816], P(None, 'req'), may hold values from -0.125 to 0.125
- shared_up: bfloat16 [2048, 2816], P(None, 'req'), may hold values from -0.125 to 0.125
- shared_down: bfloat16 [2816, 2048], P('req'), may hold values from -0.109375 to 0.109375
Outputs:
- prefill_out: bfloat16 [1024, 2048], P(('blk', 'req'))
- decode_out: bfloat16 [16, 2048], P('req')
Inputs may be any that keep to these rules, and one draw needn't show every extreme that they name: `prefill_routes`: each token names 6 different experts; every expert is named by some token; in each aligned block of 32 tokens no expert is named by more than 6 tokens, and in some block one expert is named by exactly 6. `decode_routes`: each decoded token names 6 different experts; every expert is named by some token. `cache_lengths`: some request has exactly 16384 cached positions.
All inputs are finite; a program needn't handle non-finite values. No bound on the sum of `cache_lengths` on one device may be relied on, other than what follows from the above.
Results may differ from a plain program's by a relative error of at most 0.02.
Values may be sent and summed in bfloat16 or wider, within the bound.
No kernel may reach another device: no remote copies, remote signals or barrier semaphores. Data moves between devices by JAX's collectives and lax.ppermute only.
A program may use at most 128 MiB of HBM per device.

v0:
```python
import jax
import jax.numpy as jnp
from jax import lax
from jax.sharding import PartitionSpec as P

NEG = -1e30
ROUTE_SCALE = 2.446


def merged(part, axis, combine):
    gathered = jax.tree.map(lambda a: lax.all_gather(a, axis), part)

    def take(source):
        return jax.tree.map(lambda a: lax.dynamic_index_in_dim(a, source, 0, False), gathered)

    return lax.fori_loop(
        1, lax.axis_size(axis), lambda source, state: combine(state, take(source)), take(0)
    )


def settle(values):
    return lax.optimization_barrier(values.astype(jnp.bfloat16)).astype(jnp.float32)


def rms_rows(rows_in, gain_row):
    widened = rows_in.astype(jnp.float32)
    mean_square = jnp.mean(widened * widened, axis=1, keepdims=True)
    return (widened * lax.rsqrt(mean_square + 1e-06) * gain_row).astype(jnp.bfloat16)


def swiglu(inputs, gate_w, up_w, down_w):
    gate_part = jnp.dot(inputs, gate_w, preferred_element_type=jnp.float32)
    up_part = jnp.dot(inputs, up_w, preferred_element_type=jnp.float32)
    hidden = (jax.nn.silu(gate_part) * up_part).astype(jnp.bfloat16)
    return jnp.dot(hidden, down_w, preferred_element_type=jnp.float32)


def gate_table(routes, scores, experts):
    shares = scores / jnp.sum(scores, axis=1, keepdims=True) * ROUTE_SCALE
    matches = routes[:, :, None] == jnp.arange(experts, dtype=jnp.int32)[None, None, :]
    return jnp.sum(jnp.where(matches, shares[:, :, None], 0.0), axis=1).astype(jnp.bfloat16)


def routed_terms(inputs, weight_rows, first_expert, gate_w, up_w, down_w):
    result = jnp.zeros(inputs.shape, jnp.float32)
    for slot_index in range(gate_w.shape[0]):
        weight_col = lax.dynamic_slice_in_dim(weight_rows, first_expert + slot_index, 1, 1).astype(
            jnp.float32
        )
        result = result + weight_col * swiglu(
            inputs, gate_w[slot_index], up_w[slot_index], down_w[slot_index]
        )
    return result


def merge_parts(first_part, second_part):
    row_peak = jnp.maximum(first_part[0], second_part[0])
    keep_first = jnp.exp(first_part[0] - row_peak)
    keep_second = jnp.exp(second_part[0] - row_peak)
    merged_total = first_part[1] * keep_first + second_part[1] * keep_second
    merged_sum = first_part[2] * keep_first[:, :, None] + second_part[2] * keep_second[:, :, None]
    return (row_peak, merged_total, merged_sum)


def local(
    prefill_resid,
    prefill_routes,
    prefill_scores,
    decode_resid,
    queries,
    latent_cache,
    new_latent,
    cache_lengths,
    decode_routes,
    decode_scores,
    norm_gain,
    absorb_key,
    absorb_value,
    out_proj,
    expert_gate,
    expert_up,
    expert_down,
    shared_gate,
    shared_up,
    shared_down,
):
    req_count = lax.axis_size("req")
    blk_count = lax.axis_size("blk")
    blk_index = lax.axis_index("blk")
    nope_width = absorb_key.shape[1]
    latent_width = absorb_key.shape[2]
    scale_factor = queries.shape[2] ** (-0.5)
    positions = latent_cache.shape[1]
    requests = queries.shape[0]
    head_count = queries.shape[1]
    q_latent = jnp.einsum(
        "ihn,hnl->ihl", queries[:, :, :nope_width], absorb_key, preferred_element_type=jnp.float32
    ).astype(jnp.bfloat16)
    q_full = jnp.concatenate([q_latent, queries[:, :, nope_width:]], axis=2)
    first_position = blk_index * positions
    live_mask = (first_position + jnp.arange(positions, dtype=jnp.int32))[None, :] < cache_lengths[
        :, None
    ]

    def local_part(operand):
        scores = (
            jnp.einsum("ihc,ipc->ihp", q_full, latent_cache, preferred_element_type=jnp.float32)
            * scale_factor
        )
        scores = jnp.where(live_mask[:, None, :], scores, NEG)
        row_peak = jnp.max(scores, axis=2)
        expo_weights = jnp.where(live_mask[:, None, :], jnp.exp(scores - row_peak[:, :, None]), 0.0)
        weighted = jnp.einsum(
            "ihp,ipl->ihl",
            expo_weights.astype(jnp.bfloat16),
            latent_cache[:, :, :latent_width],
            preferred_element_type=jnp.float32,
        )
        return (row_peak, jnp.sum(expo_weights, axis=2), weighted)

    def empty_part(operand):
        return (
            jnp.full((requests, head_count), NEG, jnp.float32),
            jnp.zeros((requests, head_count), jnp.float32),
            jnp.zeros((requests, head_count, latent_width), jnp.float32),
        )

    partials = lax.cond(jnp.max(cache_lengths) > first_position, local_part, empty_part, 0)
    row_peak, denominator, weighted = merged(partials, "blk", merge_parts)
    fresh_score = (
        jnp.einsum("ihc,ic->ih", q_full, new_latent, preferred_element_type=jnp.float32)
        * scale_factor
    )
    overall = jnp.maximum(row_peak, fresh_score)
    keep_old = jnp.exp(row_peak - overall)
    fresh_weight = jnp.exp(fresh_score - overall)
    denominator = denominator * keep_old + fresh_weight
    weighted = weighted * keep_old[:, :, None] + settle(fresh_weight)[:, :, None] * new_latent[
        :, None, :latent_width
    ].astype(jnp.float32)
    o_latent = (weighted / denominator[:, :, None]).astype(jnp.bfloat16)
    value_piece = lax.all_gather(absorb_value, "req", axis=0, tiled=True)
    proj_piece = lax.all_gather(out_proj, "req", axis=0, tiled=True)
    head_values = jnp.einsum(
        "ihl,hlv->ihv", o_latent, value_piece, preferred_element_type=jnp.float32
    ).astype(jnp.bfloat16)
    attention = jnp.einsum(
        "ihv,hvd->id", head_values, proj_piece, preferred_element_type=jnp.float32
    )
    hidden_dec = (decode_resid.astype(jnp.float32) + attention).astype(jnp.bfloat16)
    experts = expert_gate.shape[0] * blk_count
    first_expert = blk_index * expert_gate.shape[0]
    own_rows = jnp.concatenate(
        [rms_rows(prefill_resid, norm_gain), rms_rows(hidden_dec, norm_gain)], axis=0
    )
    own_table = jnp.concatenate(
        [
            gate_table(prefill_routes, prefill_scores, experts),
            gate_table(decode_routes, decode_scores, experts),
        ],
        axis=0,
    )
    tile_rows = own_rows.shape[0]
    model_width = own_rows.shape[1]
    every_rows, every_table = (
        lax.all_gather(own_rows, ("req", "blk"), axis=0, tiled=True),
        lax.all_gather(own_table, ("req", "blk"), axis=0, tiled=True),
    )
    grid_rows = every_rows.reshape(req_count, blk_count, tile_rows, model_width)
    column_rows = lax.dynamic_index_in_dim(grid_rows, blk_index, 1, keepdims=False).reshape(
        req_count * tile_rows, model_width
    )
    shared_column = swiglu(column_rows, shared_gate, shared_up, shared_down).reshape(
        req_count, tile_rows, model_width
    )
    routed = routed_terms(
        every_rows, every_table, first_expert, expert_gate, expert_up, expert_down
    )
    tile_ids = jnp.arange(tile_rows * lax.axis_size(("req", "blk")) // tile_rows, dtype=jnp.int32)
    in_column = tile_ids % blk_count == blk_index
    owner_rows = (tile_ids // blk_count)[:, None] == jnp.arange(req_count, dtype=jnp.int32)[None, :]
    selector = jnp.logical_and(in_column[:, None], owner_rows).astype(jnp.float32)
    shared_part = jnp.einsum(
        "tr,rnd->tnd", selector, shared_column, precision=lax.Precision.HIGHEST
    )
    moe_rows = lax.psum_scatter(
        routed + shared_part.reshape(tile_rows * lax.axis_size(("req", "blk")), model_width),
        ("req", "blk"),
        scatter_dimension=0,
        tiled=True,
    )
    prefill_count = prefill_resid.shape[0]
    prefill_out = (prefill_resid.astype(jnp.float32) + moe_rows[:prefill_count]).astype(
        jnp.bfloat16
    )
    decode_out = (hidden_dec.astype(jnp.float32) + moe_rows[prefill_count:]).astype(jnp.bfloat16)
    return (prefill_out, decode_out)


def solution(mesh):
    return jax.shard_map(
        local,
        mesh=mesh,
        in_specs=(
            P(("blk", "req"), None),
            P(("blk", "req"), None),
            P(("blk", "req"), None),
            P("req", None),
            P("req", None, None),
            P("req", "blk", None),
            P("req", None),
            P("req"),
            P("req", None),
            P("req", None),
            P(),
            P(),
            P("req", None, None),
            P("req", None, None),
            P("blk", None, "req"),
            P("blk", None, "req"),
            P("blk", "req", None),
            P(None, "req"),
            P(None, "req"),
            P("req", None),
        ),
        out_specs=(P(("blk", "req"), None), P("req", None)),
        check_vma=False,
    )
```

profile of v0, /device:TPU:2, one launch (start us, length us, event | category | flops | bytes accessed | tf_op | source)
XLA Modules:
  0.0 1075.5 jit_solution(22341837289912471)
XLA Ops:
  7.3 0.9 slice.39
  8.1 0.8 slice.40
  8.9 1.3 reduce_max.18
  11.3 3.6 conditional.1
  11.4 0.9 fusion.84
  12.4 0.7 copy.55
  13.1 1.0 fusion.1
  14.0 0.9 fusion.4
  15.6 0.7 all-gather.12.cloned.1.call-update
  16.4 0.7 all-gather.14.cloned.1.call-update
  17.1 34.3 %all-gather.5 = f32[32,2,16]{2,1,0:T(2,128)S(1)} all-gather(f32[1,2,16]{2,1,0:T(2,128)S(1)} %bitcast.96), channel_id=3, replica_groups=mesh['req'=8,'blk'=32] {'blk'}, dimensions={0}, use_global_device_ids=true | all-gather | bytes 4224 | tf_op jit(solution)/shard_map/all_gather | solution.py:11
  51.4 30.9 %all-gather.4 = f32[32,2,16]{2,1,0:T(2,128)S(1)} all-gather(f32[1,2,16]{2,1,0:T(2,128)} %bitcast.6), channel_id=2, replica_groups=mesh['req'=8,'blk'=32] {'blk'}, dimensions={0}, use_global_device_ids=true | all-gather | bytes 4224 | tf_op jit(solution)/shard_map/all_gather | solution.py:11
  82.7 0.7 all-gather.16.cloned.1.call-done
  83.4 0.8 slice.58
  84.2 30.2 %while.19 = (s32[]{:T(128)}, f32[2,16]{1,0:T(2,128)S(1)}, f32[2,16]{1,0:T(2,128)S(1)}, f32[2,16,512]{2,1,0:T(8,128)S(1)}, f32[32,2,16]{2,1,0:T(2,128)S(1)}, /*in...) while((s32[]{:T(128)}, f32[2,16]{1,0:T(2,128)S(1)}, ...), condition=%wide.region_11.12_spmd, body=%wide.region_10.11_spmd.sunk | while | flops 49349 | bytes 198039 | solution.py:16
  84.2 0.9 fusion.104
  85.2 0.9 fusion.104
  86.2 0.9 fusion.104
  87.1 0.9 fusion.104
  88.1 0.9 fusion.104
  89.1 0.9 fusion.104
  90.1 0.9 fusion.104
  91.0 0.9 fusion.104
  92.0 0.9 fusion.104
  93.0 0.9 fusion.104
  94.0 0.9 fusion.104
  94.9 0.9 fusion.104
  95.9 0.9 fusion.104
  96.9 0.9 fusion.104
  97.8 0.9 fusion.104
  98.8 0.9 fusion.104
  99.8 0.9 fusion.104
  100.8 0.9 fusion.104
  101.8 0.9 fusion.104
  102.7 0.9 fusion.104
  103.7 0.9 fusion.104
  104.7 0.9 fusion.104
  105.6 0.9 fusion.104
  106.6 0.9 fusion.104
  107.6 0.9 fusion.104
  108.6 0.9 fusion.104
  109.5 0.9 fusion.104
  110.5 0.9 fusion.104
  111.5 0.9 fusion.104
  112.5 0.9 fusion.104
  113.4 0.9 fusion.104
  114.5 30.9 %all-gather.12.cloned.1.call-done = bf16[16,512,128]{2,1,0:T(8,128)(2,1)} async-done(((bf16[2,512,128]{2,1,0:T(8,128)(2,1)}), bf16[16,512,128]{2,1,0:T(8,128)(2,1)}) %all-gather.12.cloned.1.call-update) | async-done | bytes 2097168 | tf_op jit(solution)/shard_map/all_gather | solution.py:142
  145.5 114.6 %all-gather.14.cloned.1.call-done = bf16[16,128,2048]{2,1,0:T(8,128)(2,1)} async-done(((bf16[2,128,2048]{2,1,0:T(8,128)(2,1)}), bf16[16,128,2048]{2,1,0:T(8,128)(2,1)}) %all-gather.14.cloned.1.call-update) | async-done | bytes 8388624 | tf_op jit(solution)/shard_map/all_gather | solution.py:143
  260.1 5.6 multiply_reduce_fusion
  267.5 305.6 %all-gather.3 = bf16[256,6,64]{2,1,0:T(8,128)(2,1)S(1)} all-gather(bf16[1,6,64]{2,1,0:T(8,128)(2,1)S(1)} %maximum_bitcast_fusion.1), channel_id=1, replica_groups=mesh['req'=8,'blk'=32] {'req','blk'}, dimensions={0}, use_global_device_ids=true | all-gather | bytes 197376 | tf_op jit(solution)/shard_map/all_gather | solution.py:167
  573.9 111.5 %all-gather.18.cloned.1.call-done = bf16[256,6,2048]{2,1,0:T(8,128)(2,1)} async-done(((bf16[1,6,2048]{2,1,0:T(8,128)(2,1)}), bf16[256,6,2048]{2,1,0:T(8,128)(2,1)}) %all-gather.18.cloned.1.call-update) | async-done | bytes 6291472 | tf_op jit(solution)/shard_map/all_gather | solution.py:166
  685.4 11.0 %reshape.96 = bf16[1536,2048]{1,0:T(8,128)(2,1)} reshape(bf16[256,6,2048]{2,1,0:T(8,128)(2,1)} %all-gather.18.cloned.1.call-done) | data formatting | bytes 12582912
  696.5 6.2 fusion.36
  702.7 3.2 fusion.31
  705.9 1.1 dynamic-slice_bitcast_fusion
  707.6 2.5 fusion.21
  710.2 8.1 fusion.49
  718.3 17.8 %copy.59 = f32[256,6,2048]{2,1,0:T(8,128)} copy(f32[256,6,2048]{2,0,1:T(8,128)} %fusion.49) | data formatting | bytes 25165824 | tf_op jit(solution)/shard_map/tr,rnd->tnd/dot_general | solution.py:183
  736.1 15.9 %reshape.77 = f32[1536,2048]{1,0:T(8,128)} reshape(f32[256,6,2048]{2,1,0:T(8,128)} %copy.59) | data formatting | bytes 25165824 | tf_op jit(solution)/shard_map/reshape | solution.py:187
  752.0 11.5 %fusion.19 = f32[1536,2048]{1,0:T(8,128)} fusion(bf16[1536,2048]{1,0:T(8,128)(2,1)} %reshape.96, f32[1536,176]{0,1:T(8,128)} %fusion.36, bf16[2,176,2048]{2,1,0:T(8,128)(2,1)S(1)} %copy-done.6, bf16[2,2048,176]{1,2,0:T(8,128)(2,1)S(1)} %copy-done.7), kind=kOutput, calls=%fused_computation.32 | convolution fusion | flops 2216214528 | bytes 21397504 | tf_op jit(solution)/shard_map/dot_general | solution.py:35
  763.5 17.7 %add_add_fusion = f32[1536,2048]{1,0:T(8,128)} fusion(f32[1536,2048]{1,0:T(8,128)} %reshape.77, f32[1536,2048]{1,0:T(8,128)} %fusion.19, f32[1536]{0:T(1024)S(1)} %get-tuple-element.233, f32[1536]{0:T(1024)S(1)} %get-tuple-element.232, bf16[2,176,2048]{2,1,0:T(8,128)(2,1)S(1)} %copy-done.6, bf16[1536,2048]{1,0:T(8,128)(2,1)} %reshape.96, ...), kind=kOutput, calls=%fused_computation.23 | convolution fusion | flops 2228797440 | bytes 46579712 | tf_op jit(solution)/shard_map/dot_general | solution.py:35
  781.3 284.6 %all-reduce.3.cloned.1.call-done = f32[1536,2048]{1,0:T(8,128)} async-done(((f32[1536,2048]{1,0:T(8,128)}), f32[1536,2048]{1,0:T(8,128)}) %all-reduce.3.cloned.1.call-update) | async-done | bytes 12582928
  1065.9 1.5 fusion.62
  1067.4 1.5 fusion.65
  (116 shorter events, 5.9 us)
Async XLA Ops:
  7.2 3.7 copy-start
  7.2 4.1 copy-start.18
  7.2 4.1 copy-start.3
  7.2 76.2 %all-gather.16.cloned.1.call-start = ((), (), s32[]{:S(2)}) async-start(), calls=%async_computation.2 | async-start | bytes 2162688 | tf_op jit(solution)/shard_map/all_gather | solution.py:11
  14.9 0.6 copy-start.8
  14.9 67.4 %copy-start.16 = (bf16[2,576]{1,0:T(2,128)(2,1)S(1)}, bf16[2,576]{1,0:T(2,128)(2,1)}, u32[]{:S(2)}) copy-start(bf16[2,576]{1,0:T(2,128)(2,1)} %param.30) | copy-start | bytes 6916
  14.9 67.5 %copy-start.9 = (bf16[4,2048]{1,0:T(4,128)(2,1)S(1)}, bf16[4,2048]{1,0:T(4,128)(2,1)}, u32[]{:S(2)}) copy-start(bf16[4,2048]{1,0:T(4,128)(2,1)} %param.24) | copy-start | bytes 49156
  14.9 67.7 %copy-start.11 = (f32[2048]{0:T(1024)S(1)}, f32[2048]{0:T(1024)}, u32[]{:S(2)}) copy-start(f32[2048]{0:T(1024)} %param.34) | copy-start | bytes 24580
  15.5 129.9 %all-gather.12.cloned.1.call-start = ((), (), s32[]{:S(2)}) async-start(), calls=%async_computation | async-start | bytes 2359296 | tf_op jit(solution)/shard_map/all_gather | solution.py:142
  16.3 243.8 %copy-start.12 = (bf16[2,2048]{1,0:T(2,128)(2,1)S(1)}, bf16[2,2048]{1,0:T(2,128)(2,1)}, u32[]{:S(2)}) copy-start(bf16[2,2048]{1,0:T(2,128)(2,1)} %param.27) | copy-start | bytes 24580
  16.3 243.8 %all-gather.14.cloned.1.call-start = ((), (), s32[]{:S(2)}) async-start(), calls=%async_computation.1 | async-start | bytes 9437184 | tf_op jit(solution)/shard_map/all_gather | solution.py:143
  17.0 668.4 %all-gather.18.cloned.1.call-start = ((), (), s32[]{:S(2)}) async-start(), calls=%async_computation.3 | async-start | bytes 8421376 | tf_op jit(solution)/shard_map/all_gather | solution.py:166
  114.5 152.0 %copy-start.13 = (f32[4,6]{1,0:T(4,128)S(1)}, f32[4,6]{1,0:T(4,128)}, u32[]{:S(2)}) copy-start(f32[4,6]{1,0:T(4,128)} %param.26) | copy-start | bytes 292
  114.5 152.3 %copy-start.15 = (s32[4,6]{1,0:T(4,128)S(1)}, s32[4,6]{1,0:T(4,128)}, u32[]{:S(2)}) copy-start(s32[4,6]{1,0:T(4,128)} %param.25) | copy-start | bytes 292
  114.5 152.4 %copy-start.14 = (f32[2,6]{1,0:T(2,128)S(1)}, f32[2,6]{1,0:T(2,128)}, u32[]{:S(2)}) copy-start(f32[2,6]{1,0:T(2,128)} %param.33) | copy-start | bytes 148
  114.5 152.7 %copy-start.17 = (s32[2,6]{1,0:T(2,128)S(1)}, s32[2,6]{1,0:T(2,128)}, u32[]{:S(2)}) copy-start(s32[2,6]{1,0:T(2,128)} %param.32) | copy-start | bytes 148
  266.5 799.5 %all-reduce.3.cloned.1.call-start = ((), (), s32[]{:S(2)}) async-start(), calls=%async_computation.4 | async-start | bytes 25165824
  573.9 122.6 %copy-start.19 = (bf16[2,2048,176]{1,2,0:T(8,128)(2,1)S(1)}, bf16[2,2048,176]{1,2,0:T(8,128)(2,1)}, u32[]{:S(2)}) copy-start(bf16[2,2048,176]{1,2,0:T(8,128)(2,1)} %param.38) | copy-start | bytes 4325380
  696.5 6.2 copy-start.2
  702.7 4.4 copy-start.5
  705.9 1.7 copy-start.4
  736.1 15.9 %copy-start.6 = (bf16[2,176,2048]{2,1,0:T(8,128)(2,1)S(1)}, bf16[2,176,2048]{2,1,0:T(8,128)(2,1)}, u32[]{:S(2)}) copy-start(bf16[2,176,2048]{2,1,0:T(8,128)(2,1)} %param.40) | copy-start | bytes 4325380
  736.1 15.9 %copy-start.7 = (bf16[2,2048,176]{1,2,0:T(8,128)(2,1)S(1)}, bf16[2,2048,176]{1,2,0:T(8,128)(2,1)}, u32[]{:S(2)}) copy-start(bf16[2,2048,176]{1,2,0:T(8,128)(2,1)} %param.39) | copy-start | bytes 4325380
  781.3 284.7 %copy-start.10 = (bf16[4,2048]{1,0:T(4,128)(2,1)S(1)}, bf16[4,2048]{1,0:T(4,128)(2,1)}, u32[]{:S(2)}) copy-start(bf16[4,2048]{1,0:T(4,128)(2,1)} %param.24) | copy-start | bytes 49156
  781.3 287.7 %copy-start.1 = (bf16[16,128,512]{2,1,0:T(8,128)(2,1)S(1)}, bf16[16,128,512]{2,1,0:T(8,128)(2,1)}, u32[]{:S(2)}) copy-start(bf16[16,128,512]{2,1,0:T(8,128)(2,1)} %param.35) | copy-start | bytes 6291460
Sparse Core Ops, SparseCore 0:
  15.7 67.6 all-gather.15
  86.0 59.4 all-gather.11
  148.1 111.9 all-gather.13
  266.6 418.7 all-gather.17
  781.4 284.4 all-reduce.2
where the time goes:
time: 1080 us
  waiting for transfers between devices  544 us (50%)
  blocking collectives  371 us (34%)
  matrix products  57.8 us (5%)
  local copies, waits for them, and re-layouts  50.5 us (5%)
  other arithmetic  36.9 us (3%)
  between operations  14.8 us (1%)
    all_gather x1, blocking collectives, local(): lax.all_gather(own_table, ('req', 'blk'), axis=0, tiled=True)  306 us
    unnamed x6, waiting for transfers between devices  286 us
    all_gather x1, waiting for transfers between devices, local(): proj_piece = lax.all_gather(out_proj, 'req', axis=0, tiled=True)  115 us
    all_gather x1, waiting for transfers between devices, local(): lax.all_gather(own_rows, ('req', 'blk'), axis=0, tiled=True)  112 us
    all_gather x2, blocking collectives, merged(): gathered = jax.tree.map(lambda a: lax.all_gather(a, axis), part)  65.2 us
    dot_general x3, matrix products, swiglu(): return jnp.dot(hidden, down_w, preferred_element_type=jnp.float32)  31.7 us
    all_gather x1, waiting for transfers between devices, local(): value_piece = lax.all_gather(absorb_value, 'req', axis=0, tiled=True)  30.9 us
    add x31, other arithmetic, merge_parts(): first_part[2] * keep_first[:, :, None]  28.6 us
  transfers between devices with their start and end apart: 5, of which 5 were waited for; matrix products, arithmetic and copies ran while one was open for 3% of the time, Pallas kernels for 0%

commit v1 on v0

v1 whole, which is shorter than its diff:
```python
import jax
import jax.numpy as jnp
from jax import lax
from jax.sharding import PartitionSpec as P

NEG = -1e30
ROUTE_SCALE = 2.446
CAP = 6
BF = jnp.bfloat16
F32 = jnp.float32


def exchange(payload, axis):
    return lax.all_to_all(payload, axis, 0, 0, tiled=True)


def pieces(values, count):
    parts, rest = [], values
    for _ in range(count):
        part = lax.reduce_precision(rest, 8, 7)
        parts.append(part.astype(BF))
        rest = rest - part
    return parts


def rms_rows(rows_in, gain_row):
    widened = rows_in.astype(F32)
    mean_square = jnp.mean(widened * widened, axis=1, keepdims=True)
    return (widened * lax.rsqrt(mean_square + 1e-06) * gain_row).astype(BF)


def dot(a, b):
    return jnp.dot(a, b, preferred_element_type=F32)


def swiglu(inputs, gate_w, up_w, down_w):
    hidden = (jax.nn.silu(dot(inputs, gate_w)) * dot(inputs, up_w)).astype(BF)
    return dot(hidden, down_w)


def route_row(routes, scores):
    shares = scores / jnp.sum(scores, axis=1, keepdims=True) * ROUTE_SCALE
    return jnp.concatenate([routes.astype(BF), shares.astype(BF)], axis=1)


def widen(values, width):
    return jnp.pad(values, [(0, 0)] * (values.ndim - 1) + [(0, width - values.shape[-1])])


def route_tables(rows, top, experts):
    matches = rows[:, :top].astype(jnp.int32)[:, :, None] == jnp.arange(experts, dtype=jnp.int32)
    named = jnp.sum(matches.astype(F32), axis=1)
    weight = jnp.sum(jnp.where(matches, rows[:, top : 2 * top].astype(F32)[:, :, None], 0.0), axis=1)
    return named, weight


def local(
    prefill_resid,
    prefill_routes,
    prefill_scores,
    decode_resid,
    queries,
    latent_cache,
    new_latent,
    cache_lengths,
    decode_routes,
    decode_scores,
    norm_gain,
    absorb_key,
    absorb_value,
    out_proj,
    expert_gate,
    expert_up,
    expert_down,
    shared_gate,
    shared_up,
    shared_down,
):
    req_n = lax.axis_size("req")
    blk_n = lax.axis_size("blk")
    r = lax.axis_index("req")
    b = lax.axis_index("blk")
    top = prefill_routes.shape[1]
    width = prefill_resid.shape[1]
    slice_w = width // req_n
    pre_n = prefill_resid.shape[0]
    col_n = pre_n * req_n
    own_req = decode_resid.shape[0]
    heads = queries.shape[1]
    own_heads = heads // req_n
    nope = absorb_key.shape[1]
    latent = absorb_key.shape[2]
    positions = latent_cache.shape[1]
    own_exp = expert_gate.shape[0]
    experts = own_exp * blk_n
    scale = queries.shape[2] ** (-0.5)
    part_w = latent + 128

    q_latent = jnp.einsum(
        "ihn,hnl->ihl", queries[:, :, :nope], absorb_key, preferred_element_type=F32
    ).astype(BF)
    q_full = jnp.concatenate([q_latent, queries[:, :, nope:]], axis=2)
    live = (b * positions + jnp.arange(positions, dtype=jnp.int32))[None, :] < cache_lengths[:, None]
    scores = jnp.einsum("ihc,ipc->ihp", q_full, latent_cache, preferred_element_type=F32) * scale
    scores = jnp.where(live[:, None, :], scores, NEG)
    fresh = jnp.einsum("ihc,ic->ih", q_full, new_latent, preferred_element_type=F32) * scale
    fresh = jnp.where(b == 0, fresh, NEG)
    peak = jnp.maximum(jnp.max(scores, axis=2), fresh)
    expo = jnp.where(live[:, None, :], jnp.exp(scores - peak[:, :, None]), 0.0)
    fresh_w = jnp.where(b == 0, jnp.exp(fresh - peak), 0.0)
    total = jnp.sum(expo, axis=2) + fresh_w
    summed = jnp.einsum(
        "ihp,ipl->ihl", expo.astype(BF), latent_cache[:, :, :latent], preferred_element_type=F32
    ) + fresh_w[:, :, None] * new_latent[:, None, :latent].astype(F32)
    mean = (summed / jnp.where(total > 0, total, 1.0)[:, :, None]).astype(BF)
    stats = jnp.stack(pieces(peak, 3) + pieces(total, 3), axis=-1)
    part = widen(jnp.concatenate([mean, stats], axis=-1), part_w)

    pre_row = jnp.concatenate(
        [rms_rows(prefill_resid, norm_gain), widen(route_row(prefill_routes, prefill_scores), 128)], 1
    )
    att_row = part.reshape(own_req, req_n, own_heads * part_w).transpose(1, 0, 2)
    dec_meta = jnp.broadcast_to(
        route_row(decode_routes, decode_scores)[None], (req_n, own_req, 2 * top)
    )
    att_row = widen(jnp.concatenate([att_row, dec_meta], axis=2), width + 128)
    sent = jnp.concatenate(
        [jnp.broadcast_to(pre_row[None], (req_n,) + pre_row.shape), att_row], axis=1
    )
    got = exchange(sent, "req")
    col_rows = got[:, :pre_n, :width].reshape(col_n, width)
    named, weight = route_tables(got[:, :pre_n, width:].reshape(col_n, 128), top, experts)
    pairs = got[:, pre_n:, : own_heads * part_w].reshape(blk_n, part_w)
    meta_at = own_heads * part_w
    dec_named, dec_weight = route_tables(
        got[:, pre_n:, meta_at : meta_at + 2 * top].reshape(req_n * own_req, 2 * top), top, experts
    )

    earlier = jnp.tril(jnp.ones((col_n, col_n), F32), -1)
    rank = dot(earlier, named)
    chosen = jnp.logical_and(
        named.T[:, None, :] > 0, rank.T[:, None, :] == jnp.arange(CAP, dtype=F32)[None, :, None]
    )
    mine = lax.dynamic_slice_in_dim(col_rows, r * slice_w, slice_w, 1)
    slots = jnp.einsum("est,tf->esf", chosen.astype(BF), mine, preferred_element_type=F32).astype(BF)
    sent = jnp.concatenate(
        [
            slots.reshape(blk_n, own_exp * CAP, slice_w),
            widen(pairs, 4 * slice_w).reshape(blk_n, 4, slice_w),
        ],
        axis=1,
    )
    got = exchange(sent, "blk")
    n_slot = own_exp * CAP
    slots = got[:, :n_slot].reshape(blk_n, own_exp, CAP, slice_w).transpose(1, 0, 2, 3)
    slots = slots.reshape(blk_n * n_slot, slice_w)
    part = got[:, n_slot:].reshape(blk_n, 4 * slice_w)
    peak = jnp.sum(part[:, latent : latent + 3].astype(F32), axis=1)
    total = jnp.sum(part[:, latent + 3 : latent + 6].astype(F32), axis=1)
    share = total * jnp.exp(peak - jnp.max(peak))
    o_latent = jnp.sum(share[:, None] * part[:, :latent].astype(F32), axis=0) / jnp.sum(share)
    head = b % own_heads
    request = b // own_heads
    head_value = dot(o_latent.astype(BF)[None], lax.dynamic_index_in_dim(absorb_value, head, 0, False))
    projected = dot(head_value.astype(BF), lax.dynamic_index_in_dim(out_proj, head, 0, False))[0]
    resid = lax.dynamic_index_in_dim(decode_resid, request % own_req, 0, False).astype(F32)
    owner = jnp.logical_and(request // own_req == r, head == 0)
    projected = projected + jnp.where(owner, resid, 0.0)

    sent = jnp.concatenate(
        [slots] + [p.reshape(req_n, slice_w) for p in pieces(projected, 2)], axis=0
    )
    got = exchange(jnp.broadcast_to(sent[None], (req_n,) + sent.shape), "req")
    n_all = blk_n * n_slot
    expert_rows = got[:, :n_all].transpose(1, 0, 2).reshape(own_exp, n_all // own_exp, width)
    projected = jnp.sum(got[:, n_all:].astype(F32).reshape(2 * req_n, width), axis=0)

    sent = jnp.stack(pieces(projected, 2))
    got = exchange(jnp.broadcast_to(sent[None], (blk_n,) + sent.shape), "blk")
    hidden_dec = jnp.sum(
        got.astype(F32).reshape(blk_n // own_heads, 2 * own_heads, width), axis=1
    ).astype(BF)
    dec_n = hidden_dec.shape[0]
    dec_rows = rms_rows(hidden_dec, norm_gain)

    shared_out = swiglu(
        jnp.concatenate([col_rows, dec_rows], axis=0), shared_gate, shared_up, shared_down
    )
    mask = jnp.logical_and(jnp.arange(dec_n) == request, head == 0)
    dec_sum = jnp.where(mask[:, None], shared_out[col_n:], 0.0)
    routed = []
    for k in range(own_exp):
        outs = swiglu(
            jnp.concatenate([expert_rows[k], dec_rows], axis=0),
            expert_gate[k],
            expert_up[k],
            expert_down[k],
        )
        routed.append(outs[: n_all // own_exp])
        dec_sum = dec_sum + outs[n_all // own_exp :] * lax.dynamic_slice_in_dim(
            dec_weight, b * own_exp + k, 1, 1
        )

    rows = jnp.concatenate(routed + [shared_out[:col_n]], axis=0).astype(BF)
    sent = jnp.concatenate(
        [
            rows.reshape(rows.shape[0], req_n, slice_w).transpose(1, 0, 2),
            dec_sum.astype(BF).reshape(req_n, own_req * req_n, slice_w),
        ],
        axis=1,
    )
    got = jnp.sum(exchange(sent, "req").astype(F32), axis=0)
    shared_col = got[n_all : n_all + col_n]

    back = got[:n_all].astype(BF).reshape(own_exp, blk_n, CAP, slice_w).transpose(1, 0, 2, 3)
    dec_part = got[n_all + col_n :].astype(BF)
    sent = jnp.concatenate(
        [
            back.reshape(blk_n, n_slot, slice_w),
            jnp.broadcast_to(dec_part[None], (blk_n,) + dec_part.shape),
        ],
        axis=1,
    )
    got = exchange(sent, "blk")
    dec_total = jnp.sum(got[:, n_slot:].astype(F32), axis=0).reshape(own_req, width)
    table = jnp.where(chosen, weight.T[:, None, :], 0.0).astype(BF)
    col_sum = shared_col + jnp.einsum(
        "est,esf->tf",
        table,
        got[:, :n_slot].reshape(experts, CAP, slice_w),
        preferred_element_type=F32,
    )

    got = exchange(col_sum.reshape(req_n, pre_n, slice_w), "req")
    own_sum = got.transpose(1, 0, 2).reshape(pre_n, width)
    prefill_out = (prefill_resid.astype(F32) + own_sum).astype(BF)
    own_dec = lax.dynamic_slice_in_dim(hidden_dec, r * own_req, own_req, 0)
    decode_out = (own_dec.astype(F32) + dec_total).astype(BF)
    return (prefill_out, decode_out)


def solution(mesh):
    return jax.shard_map(
        local,
        mesh=mesh,
        in_specs=(
            P(("blk", "req"), None),
            P(("blk", "req"), None),
            P(("blk", "req"), None),
            P("req", None),
            P("req", None, None),
            P("req", "blk", None),
            P("req", None),
            P("req"),
            P("req", None),
            P("req", None),
            P(),
            P(),
            P("req", None, None),
            P("req", None, None),
            P("blk", None, "req"),
            P("blk", None, "req"),
            P("blk", "req", None),
            P(None, "req"),
            P(None, "req"),
            P("req", None),
        ),
        out_specs=(P(("blk", "req"), None), P("req", None)),
        check_vma=False,
    )
```

time: 1080 us -> 194 us (0.18)
  waiting for transfers between devices: 544 us -> 73.8 us
  blocking collectives: 371 us -> 29.6 us
  matrix products: 57.8 us -> 20.8 us
  starting transfers between devices: 0.2 us -> 33.9 us
  local copies, waits for them, and re-layouts: 50.5 us -> 17.3 us
  other arithmetic: 36.9 us -> 15.8 us
  between operations: 14.8 us -> 1.4 us
    all_gather x3 -> x0, blocking collectives: 371 us -> none  [the longest x1 306 us: local(): lax.all_gather(own_table, ('req', 'blk'), axis=0, tiled=True)]
    unnamed x6 -> x0, waiting for transfers between devices: 286 us -> none
    all_gather x4 -> x0, waiting for transfers between devices: 258 us -> none  [the longest x1 115 us: local(): proj_piece = lax.all_gather(out_proj, 'req', axis=0, tiled=True)]
    all_to_all x0 -> x6, waiting for transfers between devices: none -> 73.8 us  [exchange(): return lax.all_to_all(payload, axis, 0, 0, tiled=True)]
    dot_general x12 -> x14, matrix products: 57.8 us -> 20.8 us  [the longest x8 18.1 us: dot(): return jnp.dot(a, b, preferred_element_type=F32)]
    all_to_all x0 -> x6, starting transfers between devices: none -> 33.9 us  [exchange(): return lax.all_to_all(payload, axis, 0, 0, tiled=True)]
    all_to_all x0 -> x1, blocking collectives: none -> 29.6 us  [exchange(): return lax.all_to_all(payload, axis, 0, 0, tiled=True)]
    add x64 -> x2, other arithmetic: 29.4 us -> 0.01 us  [the longest x1 0.01 us: local(): b * positions + jnp.arange(positions, dtype=jnp.int32)]
  transfers between devices with their start and end apart: 5 -> 6, of which waited for: 5 -> 6; matrix products, arithmetic and copies ran while one was open for 3% -> 4% of each run, Pallas kernels for 0% -> 0%
where the time goes in v1:
time: 194 us; the launch traced here: 193 us
  waiting for transfers between devices  73.8 us (38%)
  starting transfers between devices  33.9 us (17%)
  blocking collectives  29.6 us (15%)
  matrix products  20.8 us (11%)
  local copies, waits for them, and re-layouts  17.3 us (9%)
  other arithmetic  15.8 us (8%)
    all_to_all x6, waiting for transfers between devices, exchange(): return lax.all_to_all(payload, axis, 0, 0, tiled=True)  73.8 us
    all_to_all x6, starting transfers between devices, exchange(): return lax.all_to_all(payload, axis, 0, 0, tiled=True)  33.9 us
    all_to_all x1, blocking collectives, exchange(): return lax.all_to_all(payload, axis, 0, 0, tiled=True)  29.6 us
    dot_general x8, matrix products, dot(): return jnp.dot(a, b, preferred_element_type=F32)  18.1 us
  transfers between devices with their start and end apart: 6, of which 6 were waited for; matrix products, arithmetic and copies ran while one was open for 4% of the time, Pallas kernels for 0%

profile of v1, /device:TPU:2, one launch (start us, length us, event | category | flops | bytes accessed | tf_op | source)
XLA Modules:
  0.0 192.6 jit_solution(14201181714782465504)
XLA Ops:
  0.7 0.9 slice.122
  1.5 0.8 slice.121
  2.4 0.8 reduce_sum.156
  3.2 0.8 multiply_convert_fusion.1
  3.9 0.7 convert_element_type.194
  4.6 0.7 slice_convert_fusion.4
  5.3 0.4 fusion.9
  5.9 0.1 fusion.77
  6.0 0.4 fusion.139
  6.4 0.2 fusion.68
  7.2 0.4 fusion.7
  8.1 0.1 fusion.80
  8.5 0.8 fusion.36
  9.3 7.5 %all-to-all-start = ((bf16[8,6,2176]{2,1,0:T(8,128)(2,1)}), bf16[8,6,2176]{2,1,0:T(8,128)(2,1)S(1)}, u32[]{:S(2)}, u32[]{:S(2)}) async-start(bf16[8,6,2176]{2,1,0:T(8,128)(2,1)} %fusion.36), calls=%async_computation | async-start | bytes 557056 | tf_op jit(solution)/shard_map/all_to_all | solution.py:14
  16.8 7.8 %all-to-all-done = bf16[8,6,2176]{2,1,0:T(8,128)(2,1)S(1)} async-done(((bf16[8,6,2176]{2,1,0:T(8,128)(2,1)}), bf16[8,6,2176]{2,1,0:T(8,128)(2,1)S(1)}, u32[]{:S(2)}, u32[]{:S(2)}) %all-to-all-start) | async-done | bytes 208928 | tf_op jit(solution)/shard_map/all_to_all | solution.py:14
  25.0 0.7 select_reduce_fusion
  25.7 0.2 fusion.90
  26.0 0.3 convolution_convert_fusion
  26.5 0.8 pad_maximum_fusion.10
  27.3 9.0 %all-to-all-start.1 = ((bf16[32,16,256]{2,1,0:T(8,128)(2,1)}), bf16[32,16,256]{2,1,0:T(8,128)(2,1)S(1)}, u32[]{:S(2)}, u32[]{:S(2)}) async-start(bf16[32,16,256]{2,1,0:T(8,128)(2,1)} %pad_maximum_fusion.10), calls=%async_computation.1 | async-start | bytes 524288 | tf_op jit(solution)/shard_map/all_to_all | solution.py:14
  36.4 1.1 constant_dynamic-slice_fusion
  37.5 11.9 %all-to-all-done.1 = bf16[32,16,256]{2,1,0:T(8,128)(2,1)S(1)} async-done(((bf16[32,16,256]{2,1,0:T(8,128)(2,1)}), bf16[32,16,256]{2,1,0:T(8,128)(2,1)S(1)}, u32[]{:S(2)}, u32[]{:S(2)}) %all-to-all-start.1) | async-done | bytes 262176 | tf_op jit(solution)/shard_map/all_to_all | solution.py:14
  49.5 0.2 convert_reduce_fusion.4
  49.6 0.6 reduce_max.19
  50.3 1.2 fusion.135
  51.6 0.6 divide_convert_fusion
  52.5 1.2 fusion.32
  53.8 1.3 broadcast_in_dim.156
  55.0 5.3 %all-to-all-start.2 = ((bf16[8,400,256]{2,1,0:T(8,128)(2,1)}), bf16[8,400,256]{2,1,0:T(8,128)(2,1)}, u32[]{:S(2)}, u32[]{:S(2)}) async-start(bf16[8,400,256]{2,1,0:T(8,128)(2,1)} %broadcast_in_dim.156), calls=%async_computation.2 | async-start | bytes 3276800 | tf_op jit(solution)/shard_map/all_to_all | solution.py:14
  60.4 0.6 compare_and_fusion
  61.4 0.7 dynamic-slice_reduce_fusion.1
  62.1 20.2 %all-to-all-done.2 = bf16[8,400,256]{2,1,0:T(8,128)(2,1)} async-done(((bf16[8,400,256]{2,1,0:T(8,128)(2,1)}), bf16[8,400,256]{2,1,0:T(8,128)(2,1)}, u32[]{:S(2)}, u32[]{:S(2)}) %all-to-all-start.2) | async-done | bytes 1638432 | tf_op jit(solution)/shard_map/all_to_all | solution.py:14
  82.3 0.9 slice_convert_fusion.3
  83.3 0.8 broadcast_in_dim.157
  84.2 3.9 %all-to-all-start.3 = ((bf16[32,2,2048]{2,1,0:T(2,128)(2,1)}), bf16[32,2,2048]{2,1,0:T(2,128)(2,1)S(1)}, u32[]{:S(2)}, u32[]{:S(2)}) async-start(bf16[32,2,2048]{2,1,0:T(2,128)(2,1)} %broadcast_in_dim.157), calls=%async_computation.3 | async-start | bytes 524288 | tf_op jit(solution)/shard_map/all_to_all | solution.py:14
  88.0 1.5 slice_bitcast_fusion
  89.8 1.0 copy.228
  90.8 10.5 %all-to-all-done.3 = bf16[32,2,2048]{2,1,0:T(2,128)(2,1)S(1)} async-done(((bf16[32,2,2048]{2,1,0:T(2,128)(2,1)}), bf16[32,2,2048]{2,1,0:T(2,128)(2,1)S(1)}, u32[]{:S(2)}, u32[]{:S(2)}) %all-to-all-start.3) | async-done | bytes 262176 | tf_op jit(solution)/shard_map/all_to_all | solution.py:14
  101.3 0.1 reduce_sum.165
  101.4 0.3 reduce_sum.166
  101.8 0.1 fusion.48
  102.1 2.4 %fusion.17 = f32[208,176]{0,1:T(8,128)} fusion(bf16[2,2048,176]{1,2,0:T(8,128)(2,1)} %param.34, bf16[16,2048]{1,0:T(8,128)(2,1)S(1)} %fusion.50, bf16[192,2048]{1,0:T(8,128)(2,1)S(1)} %bitcast.125), kind=kOutput, calls=%fused_computation.37 | convolution fusion | flops 151650304 | bytes 1719296 | tf_op jit(solution)/shard_map/dot_general | solution.py:33
  104.4 0.4 fusion.22
  104.9 3.8 %fusion.2 = f32[208,2048]{1,0:T(8,128)} fusion(bf16[2,176,2048]{2,1,0:T(8,128)(2,1)} %param.36, bf16[2,2048,176]{1,2,0:T(8,128)(2,1)} %param.35, bf16[16,2048]{1,0:T(8,128)(2,1)S(1)} %fusion.50, bf16[192,2048]{1,0:T(8,128)(2,1)S(1)} %bitcast.126, f32[208,176]{0,1:T(8,128)} %fusion.17), kind=kOutput, calls=%fused_computation.13 | convolution fusion | flops 301816320 | bytes 4177920 | tf_op jit(solution)/shard_map/dot_general | solution.py:33
  108.7 3.9 %fusion.3 = f32[208,2048]{1,0:T(8,128)} fusion(bf16[2,176,2048]{2,1,0:T(8,128)(2,1)} %param.36, bf16[2,2048,176]{1,2,0:T(8,128)(2,1)} %param.35, bf16[16,2048]{1,0:T(8,128)(2,1)S(1)} %fusion.50, bf16[192,2048]{1,0:T(8,128)(2,1)} %bitcast.127, f32[208,176]{0,1:T(8,128)S(1)} %fusion.22), kind=kOutput, calls=%fused_computation.14 | convolution fusion | flops 301816320 | bytes 4144128 | tf_op jit(solution)/shard_map/dot_general | solution.py:33
  112.7 2.8 %fusion.58 = f32[48,352]{1,0:T(8,128)} fusion(bf16[2048,352]{0,1:T(8,128)(2,1)} %param.37, bf16[16,2048]{1,0:T(8,128)(2,1)} %copy-done.6, bf16[32,2048]{1,0:T(8,128)(2,1)} %copy-done.2), kind=kOutput, calls=%fused_computation.87 | convolution fusion | flops 69599232 | bytes 1705984 | tf_op jit(solution)/shard_map/dot_general | solution.py:33
  115.4 3.4 %fusion.8 = f32[48,2048]{1,0:T(8,128)} fusion(bf16[352,2048]{1,0:T(8,128)(2,1)S(1)} %copy-done.1, bf16[2048,352]{0,1:T(8,128)(2,1)} %param.38, bf16[16,2048]{1,0:T(8,128)(2,1)} %copy-done.6, bf16[32,2048]{1,0:T(8,128)(2,1)} %copy-done.2, f32[48,352]{1,0:T(8,128)} %fusion.58), kind=kOutput, calls=%fused_computation.23 | convolution fusion | flops 138906624 | bytes 3540992 | tf_op jit(solution)/shard_map/dot_general | solution.py:33
  118.8 1.1 slice.243
  119.9 1.5 slice.241
  121.4 1.0 slice.242
  122.4 1.1 fusion.52
  123.6 1.3 copy_bitcast_fusion
  125.1 29.6 %all_to_all.35 = bf16[8,432,256]{2,1,0:T(8,128)(2,1)S(1)} all-to-all(bf16[8,432,256]{2,1,0:T(8,128)(2,1)S(1)} %pad_maximum_fusion), channel_id=1, replica_groups=mesh['req'=8,'blk'=32] {'req'}, dimensions={0} | all-to-all | bytes 3538944 | tf_op jit(solution)/shard_map/all_to_all | solution.py:14
  154.7 0.2 convert_reduce_fusion
  155.3 0.9 pad_maximum_fusion.9
  156.2 3.9 %all-to-all-start.5 = ((bf16[32,28,256]{2,1,0:T(8,128)(2,1)}), bf16[32,28,256]{2,1,0:T(8,128)(2,1)S(1)}, u32[]{:S(2)}, u32[]{:S(2)}) async-start(bf16[32,28,256]{2,1,0:T(8,128)(2,1)} %pad_maximum_fusion.9), calls=%async_computation.5 | async-start | bytes 1048576 | tf_op jit(solution)/shard_map/all_to_all | solution.py:14
  160.1 18.5 %all-to-all-done.5 = bf16[32,28,256]{2,1,0:T(8,128)(2,1)S(1)} async-done(((bf16[32,28,256]{2,1,0:T(8,128)(2,1)}), bf16[32,28,256]{2,1,0:T(8,128)(2,1)S(1)}, u32[]{:S(2)}, u32[]{:S(2)}) %all-to-all-start.5) | async-done | bytes 458784 | tf_op jit(solution)/shard_map/all_to_all | solution.py:14
  178.6 0.8 reshape.208
  179.4 1.1 fusion.10
  180.5 0.6 reshape.209
  181.1 4.4 %all-to-all-start.6 = ((f32[8,4,256]{2,1,0:T(4,128)}), f32[8,4,256]{2,1,0:T(4,128)S(1)}, u32[]{:S(2)}, u32[]{:S(2)}) async-start(f32[8,4,256]{2,1,0:T(4,128)} %reshape.209), calls=%async_computation.6 | async-start | bytes 65536 | tf_op jit(solution)/shard_map/all_to_all | solution.py:14
  185.7 1.4 add_convert_fusion
  187.0 4.9 %all-to-all-done.6 = f32[8,4,256]{2,1,0:T(4,128)S(1)} async-done(((f32[8,4,256]{2,1,0:T(4,128)}), f32[8,4,256]{2,1,0:T(4,128)S(1)}, u32[]{:S(2)}, u32[]{:S(2)}) %all-to-all-start.6) | async-done | bytes 32800 | tf_op jit(solution)/shard_map/all_to_all | solution.py:14
  192.0 0.6 fusion.83
  (133 shorter events, 4.3 us)
Async XLA Ops:
  0.6 4.7 %copy-start = (bf16[16,128,512]{2,1,0:T(8,128)(2,1)S(1)}, bf16[16,128,512]{2,1,0:T(8,128)(2,1)}, u32[]{:S(2)}) copy-start(bf16[16,128,512]{2,1,0:T(8,128)(2,1)} %param.31) | copy-start | bytes 6291460
  0.6 5.2 %copy-start.20 = (bf16[2,576]{1,0:T(2,128)(2,1)S(1)}, bf16[2,576]{1,0:T(2,128)(2,1)}, u32[]{:S(2)}) copy-start(bf16[2,576]{1,0:T(2,128)(2,1)} %param.26) | copy-start | bytes 6916
  0.7 5.1 %copy-start.21 = (s32[2]{0:T(128)S(1)}, s32[2]{0:T(128)}, u32[]{:S(2)}) copy-start(s32[2]{0:T(128)} %param.27) | copy-start | bytes 28
  0.7 5.3 %copy-start.3 = (bf16[2,512,576]{1,2,0:T(8,128)(2,1)S(1)}, bf16[2,512,576]{1,2,0:T(8,128)(2,1)}, u32[]{:S(2)}) copy-start(bf16[2,512,576]{1,2,0:T(8,128)(2,1)} %param.25) | copy-start | bytes 3538948
  5.8 2.0 %copy-start.14 = (f32[4,6]{1,0:T(4,128)S(1)}, f32[4,6]{1,0:T(4,128)}, u32[]{:S(2)}) copy-start(f32[4,6]{1,0:T(4,128)} %param.22) | copy-start | bytes 292
  5.8 2.2 %copy-start.17 = (s32[4,6]{1,0:T(4,128)S(1)}, s32[4,6]{1,0:T(4,128)}, u32[]{:S(2)}) copy-start(s32[4,6]{1,0:T(4,128)} %param.21) | copy-start | bytes 292
  5.8 2.3 %copy-start.8 = (bf16[4,2048]{1,0:T(4,128)(2,1)S(1)}, bf16[4,2048]{1,0:T(4,128)(2,1)}, u32[]{:S(2)}) copy-start(bf16[4,2048]{1,0:T(4,128)(2,1)} %param.20) | copy-start | bytes 49156
  6.0 2.3 %copy-start.9 = (f32[2048]{0:T(1024)S(1)}, f32[2048]{0:T(1024)}, u32[]{:S(2)}) copy-start(f32[2048]{0:T(1024)} %param.30) | copy-start | bytes 24580
  9.3 15.2 %all-to-all-start = ((bf16[8,6,2176]{2,1,0:T(8,128)(2,1)}), bf16[8,6,2176]{2,1,0:T(8,128)(2,1)S(1)}, u32[]{:S(2)}, u32[]{:S(2)}) async-start(bf16[8,6,2176]{2,1,0:T(8,128)(2,1)} %fusion.36), calls=%async_computation | async-start | bytes 557056 | tf_op jit(solution)/shard_map/all_to_all | solution.py:14
  24.6 11.7 %copy-start.15 = (bf16[2,2048]{1,0:T(2,128)(2,1)S(1)}, bf16[2,2048]{1,0:T(2,128)(2,1)}, u32[]{:S(2)}) copy-start(bf16[2,2048]{1,0:T(2,128)(2,1)} %param.23) | copy-start | bytes 24580
  25.7 11.7 %copy-start.12 = (pred[64,32]{0,1:T(8,128)(4,1)}, pred[64,32]{0,1:T(8,128)(4,1)S(1)}, u32[]{:S(2)}) copy-start(pred[64,32]{0,1:T(8,128)(4,1)S(1)} %compare_bitcast_fusion) | copy-start | bytes 6148
  25.9 11.5 %copy-start.10 = (f32[64,32]{0,1:T(8,128)}, f32[64,32]{0,1:T(8,128)S(1)}, u32[]{:S(2)}) copy-start(f32[64,32]{0,1:T(8,128)S(1)} %fusion.90) | copy-start | bytes 24580
  26.0 10.3 %copy-start.2 = (bf16[32,2048]{1,0:T(8,128)(2,1)}, bf16[32,2048]{1,0:T(8,128)(2,1)S(1)}, u32[]{:S(2)}) copy-start(bf16[32,2048]{1,0:T(8,128)(2,1)S(1)} %reshape.195) | copy-start | bytes 393220
  27.3 22.2 %all-to-all-start.1 = ((bf16[32,16,256]{2,1,0:T(8,128)(2,1)}), bf16[32,16,256]{2,1,0:T(8,128)(2,1)S(1)}, u32[]{:S(2)}, u32[]{:S(2)}) async-start(bf16[32,16,256]{2,1,0:T(8,128)(2,1)} %pad_maximum_fusion.10), calls=%async_computation.1 | async-start | bytes 524288 | tf_op jit(solution)/shard_map/all_to_all | solution.py:14
  55.0 27.3 %all-to-all-start.2 = ((bf16[8,400,256]{2,1,0:T(8,128)(2,1)}), bf16[8,400,256]{2,1,0:T(8,128)(2,1)}, u32[]{:S(2)}, u32[]{:S(2)}) async-start(bf16[8,400,256]{2,1,0:T(8,128)(2,1)} %broadcast_in_dim.156), calls=%async_computation.2 | async-start | bytes 3276800 | tf_op jit(solution)/shard_map/all_to_all | solution.py:14
  84.2 17.1 %all-to-all-start.3 = ((bf16[32,2,2048]{2,1,0:T(2,128)(2,1)}), bf16[32,2,2048]{2,1,0:T(2,128)(2,1)S(1)}, u32[]{:S(2)}, u32[]{:S(2)}) async-start(bf16[32,2,2048]{2,1,0:T(2,128)(2,1)} %broadcast_in_dim.157), calls=%async_computation.3 | async-start | bytes 524288 | tf_op jit(solution)/shard_map/all_to_all | solution.py:14
  101.8 3.1 %copy-start.5 = (bf16[16,2048]{1,0:T(8,128)(2,1)}, bf16[16,2048]{1,0:T(8,128)(2,1)S(1)}, u32[]{:S(2)}) copy-start(bf16[16,2048]{1,0:T(8,128)(2,1)S(1)} %reduce_sum.166) | copy-start | bytes 196612
  101.8 2.7 %copy-start.4 = (bf16[8,24,8,256]{3,2,0,1:T(8,128)(2,1)S(1)}, bf16[8,24,8,256]{3,2,0,1:T(8,128)(2,1)}, u32[]{:S(2)}) copy-start(bf16[8,24,8,256]{3,2,0,1:T(8,128)(2,1)} %copy.228) | copy-start | bytes 2359300
  101.8 2.7 %copy-start.23 = (bf16[2,2048,176]{1,2,0:T(8,128)(2,1)S(1)}, bf16[2,2048,176]{1,2,0:T(8,128)(2,1)}, u32[]{:S(2)}) copy-start(bf16[2,2048,176]{1,2,0:T(8,128)(2,1)} %param.34) | copy-start | bytes 4325380
  102.0 6.7 %copy-start.6 = (bf16[16,2048]{1,0:T(8,128)(2,1)}, bf16[16,2048]{1,0:T(8,128)(2,1)S(1)}, u32[]{:S(2)}) copy-start(bf16[16,2048]{1,0:T(8,128)(2,1)S(1)} %fusion.50) | copy-start | bytes 196612
  112.7 2.8 %copy-start.1 = (bf16[352,2048]{1,0:T(8,128)(2,1)S(1)}, bf16[352,2048]{1,0:T(8,128)(2,1)}, u32[]{:S(2)}) copy-start(bf16[352,2048]{1,0:T(8,128)(2,1)} %param.39) | copy-start | bytes 4325380
  118.8 2.6 %copy-start.7 = (f32[208,2048]{1,0:T(8,128)S(1)}, f32[208,2048]{1,0:T(8,128)}, u32[]{:S(2)}) copy-start(f32[208,2048]{1,0:T(8,128)} %fusion.3) | copy-start | bytes 5111812
  118.8 3.6 %copy-start.18 = (f32[16]{0:T(128)S(1)}, f32[16]{0:T(128)}, u32[]{:S(2)}) copy-start(f32[16]{0:T(128)} %get-tuple-element.4) | copy-start | bytes 196
  118.8 3.6 %copy-start.19 = (f32[16]{0:T(128)S(1)}, f32[16]{0:T(128)}, u32[]{:S(2)}) copy-start(f32[16]{0:T(128)} %get-tuple-element.5) | copy-start | bytes 196
  118.8 3.6 %copy-start.22 = (pred[16]{0:T(512)(128)(4,1)S(1)}, pred[16]{0:T(512)(128)(4,1)}, u32[]{:S(2)}) copy-start(pred[16]{0:T(512)(128)(4,1)} %compare_and_fusion) | copy-start | bytes 52
  155.2 24.1 %copy-start.11 = (f32[64,32]{0,1:T(8,128)S(1)}, f32[64,32]{0,1:T(8,128)}, u32[]{:S(2)}) copy-start(f32[64,32]{0,1:T(8,128)} %copy-done.10) | copy-start | bytes 24580
  155.2 24.1 %copy-start.13 = (pred[64,32]{0,1:T(8,128)(4,1)S(1)}, pred[64,32]{0,1:T(8,128)(4,1)}, u32[]{:S(2)}) copy-start(pred[64,32]{0,1:T(8,128)(4,1)} %copy-done.12) | copy-start | bytes 6148
  155.2 24.1 %copy-start.16 = (bf16[32,64]{1,0:T(8,128)(2,1)S(1)}, bf16[32,64]{1,0:T(8,128)(2,1)}, u32[]{:S(2)}) copy-start(bf16[32,64]{1,0:T(8,128)(2,1)} %get-tuple-element.6) | copy-start | bytes 12292
  156.2 22.4 %all-to-all-start.5 = ((bf16[32,28,256]{2,1,0:T(8,128)(2,1)}), bf16[32,28,256]{2,1,0:T(8,128)(2,1)S(1)}, u32[]{:S(2)}, u32[]{:S(2)}) async-start(bf16[32,28,256]{2,1,0:T(8,128)(2,1)} %pad_maximum_fusion.9), calls=%async_computation.5 | async-start | bytes 1048576 | tf_op jit(solution)/shard_map/all_to_all | solution.py:14
  181.1 10.8 %all-to-all-start.6 = ((f32[8,4,256]{2,1,0:T(4,128)}), f32[8,4,256]{2,1,0:T(4,128)S(1)}, u32[]{:S(2)}, u32[]{:S(2)}) async-start(f32[8,4,256]{2,1,0:T(4,128)} %reshape.209), calls=%async_computation.6 | async-start | bytes 65536 | tf_op jit(solution)/shard_map/all_to_all | solution.py:14

commit v2 on v0

v2 whole, which is shorter than its diff:
```python
import jax
import jax.numpy as jnp
from jax import lax
from jax.experimental import pallas as pl
from jax.experimental.pallas import tpu as pltpu
from jax.sharding import PartitionSpec as P

NEG = -1e30
ROUTE_SCALE = 2.446
CAP = 6
BF = jnp.bfloat16
F32 = jnp.float32
I32 = jnp.int32
VMEM = pl.BlockSpec(memory_space=pltpu.VMEM)
SMEM = pl.BlockSpec(memory_space=pltpu.SMEM)


def exchange(payload, axis):
    return lax.all_to_all(payload, axis, 0, 0, tiled=True)


def dot(a, b):
    return jnp.dot(a, b, preferred_element_type=F32)


def dot_t(a, b):
    return lax.dot_general(a, b, (((1,), (1,)), ((), ())), preferred_element_type=F32)


def iota(shape, dim):
    return lax.broadcasted_iota(I32, shape, dim)


def bits(mask):
    return jnp.where(mask, 1.0, 0.0).astype(BF)


def rounded(values):
    return values.astype(BF).astype(F32)


def pieces(values):
    first = rounded(values)
    second = rounded(values - first)
    return [first, second, values - first - second]


def silu_mul(gate, up):
    return (gate * jax.nn.sigmoid(gate) * up).astype(BF)


def slot_of(row):
    place = row & 15
    second = (place >= CAP).astype(I32)
    return row >> 4, place, second, place - CAP * second


def start_kernel(*refs):
    count = (len(refs) - 2) // 2
    sources, out_ref, held, sems = refs[:count], refs[count], refs[count + 1 : -1], refs[-1]
    copies = [pltpu.make_async_copy(s, h, sems.at[n]) for n, (s, h) in enumerate(zip(sources, held))]
    for copy in copies:
        copy.start()
    q_ref, key_ref, res_ref, gain_ref, prt_ref, psc_ref, drt_ref, dsc_ref, new_ref, len_ref, cache_ref = held
    b = lax.axis_index("blk")
    for copy in copies[2:8]:
        copy.wait()
    pre_n, width = res_ref.shape
    n_req, heads, qw = q_ref.shape
    _, nope, latent = key_ref.shape
    positions = cache_ref.shape[2]
    scale = qw ** (-0.5)

    x = res_ref[...].astype(F32)
    mean_square = jnp.mean(x * x, axis=1, keepdims=True)
    rows = x * lax.rsqrt(mean_square + 1e-06) * gain_ref[...]

    def shares(sc):
        return rounded(sc / jnp.sum(sc, axis=1, keepdims=True) * ROUTE_SCALE)

    lane = iota((pre_n, 128), 1)
    row = iota((pre_n, 128), 0)
    top = prt_ref.shape[1]
    pr, ps = prt_ref[...].astype(F32), shares(psc_ref[...])
    dr, ds = drt_ref[...].astype(F32), shares(dsc_ref[...])
    meta = jnp.zeros((pre_n, 128), F32)
    for k in range(top):
        meta = jnp.where(lane == k, pr[:, k : k + 1], meta)
        meta = jnp.where(lane == top + k, ps[:, k : k + 1], meta)
        for i in range(n_req):
            at = jnp.logical_and(row == 2 * i, lane == 16 + k)
            meta = jnp.where(at, dr[i : i + 1, k : k + 1], meta)
            at = jnp.logical_and(row == 2 * i, lane == 16 + top + k)
            meta = jnp.where(at, ds[i : i + 1, k : k + 1], meta)

    for copy in copies[:2]:
        copy.wait()
    q_all = jnp.concatenate([q_ref[i] for i in range(n_req)], axis=0)
    q_nope = q_all[:, :nope]
    q_rope = q_all[:, nope:]
    q_head = iota((n_req * heads, latent), 0) & (heads - 1)
    q_lat = jnp.zeros((n_req * heads, latent), F32)
    for h in range(heads):
        q_lat = jnp.where(q_head == h, dot(q_nope, key_ref[h]), q_lat)
    q_lat = q_lat.astype(BF)

    for copy in copies[8:]:
        copy.wait()
    fresh_rows = new_ref[...].astype(F32)
    first = b == 0
    parts = []
    for i in range(n_req):
        ql = q_lat[i * heads : (i + 1) * heads]
        qr = q_rope[i * heads : (i + 1) * heads]
        s = (dot(ql, cache_ref[i, :latent, :]) + dot(qr, cache_ref[i, latent:, :])) * scale
        live = b * positions + iota((heads, positions), 1) < len_ref[i]
        s = jnp.where(live, s, NEG)
        new = fresh_rows[i : i + 1]
        fresh = jnp.sum(ql.astype(F32) * new[:, :latent], axis=1, keepdims=True)
        fresh = (fresh + jnp.sum(qr.astype(F32) * new[:, latent:], axis=1, keepdims=True)) * scale
        fresh = jnp.where(first, fresh, NEG)
        peak = jnp.maximum(jnp.max(s, axis=1, keepdims=True), fresh)
        expo = jnp.where(live, jnp.exp(s - peak), 0.0)
        fresh_w = jnp.where(first, jnp.exp(fresh - peak), 0.0)
        total = jnp.sum(expo, axis=1, keepdims=True) + fresh_w
        summed = dot_t(expo.astype(BF), cache_ref[i, :latent, :]) + rounded(fresh_w) * new[:, :latent]
        mean = summed / jnp.where(total > 0.0, total, 1.0)
        lane_h = iota((heads, 128), 1)
        stats = jnp.zeros((heads, 128), F32)
        for k, piece in enumerate(pieces(peak) + pieces(total)):
            stats = jnp.where(lane_h == k, piece, stats)
        parts.append(jnp.concatenate([mean, stats], axis=1))

    own = heads // out_ref.shape[0]
    for d in range(out_ref.shape[0]):
        att = jnp.concatenate([p[own * d : own * (d + 1)] for p in parts], axis=0)
        out_ref[d] = jnp.concatenate([rows, meta, att], axis=1).astype(BF)


def route_kernel(got_ref, send_ref, cols_ref, comb_ref, decw_ref):
    r = lax.axis_index("req")
    b = lax.axis_index("blk")
    n_src, pre_n, _ = got_ref.shape
    col_n, width = cols_ref.shape
    slice_w = send_ref.shape[2]
    blk_n = send_ref.shape[0]
    experts = 2 * blk_n
    top = 6
    full = jnp.concatenate([got_ref[s].astype(F32) for s in range(n_src)], axis=0)
    cols_ref[...] = full[:, :width].astype(BF)
    meta = full[:, width : width + 128]
    pairs = full[:, width + 128 :]

    expert = iota((col_n, experts), 1).astype(F32)
    named = jnp.zeros((col_n, experts), F32)
    weight = jnp.zeros((col_n, experts), F32)
    for k in range(top):
        hit = meta[:, k : k + 1] == expert
        named = jnp.where(hit, 1.0, named)
        weight = jnp.where(hit, meta[:, top + k : top + k + 1], weight)
    earlier = bits(iota((col_n, col_n), 1) < iota((col_n, col_n), 0))
    rank = dot(earlier, named.astype(BF))
    value = jnp.where(named > 0.0, rank + 1.0, 0.0)

    n_row = blk_n * 16
    column, place, second, slot = slot_of(iota((n_row, experts), 0))
    picks = jnp.logical_and(iota((n_row, experts), 1) == 2 * column + second, place < 2 * CAP)
    picks = bits(picks)
    rest = jnp.zeros((128 - col_n, experts), F32)
    value = dot_t(picks, jnp.concatenate([value, rest], axis=0).astype(BF))
    weight = dot_t(picks, jnp.concatenate([weight, rest], axis=0).astype(BF))
    row = iota((n_row, 128), 0)
    lane = iota((n_row, 128), 1)
    _, _, _, slot = slot_of(row)
    chosen = value == (slot + 1).astype(F32)
    comb_ref[...] = jnp.where(chosen, weight, 0.0).astype(BF)
    carried = jnp.logical_and(lane >= col_n, row == (lane & (col_n - 1)) * 16 + 11 + (lane >> 5))
    mine = cols_ref[:, pl.ds(pl.multiple_of(r * slice_w, slice_w), slice_w)]
    last = jnp.concatenate([pairs[:, 2 * slice_w :], jnp.zeros((col_n, slice_w - 128), F32)], axis=1)
    data = jnp.concatenate(
        [mine, pairs[:, :slice_w].astype(BF), pairs[:, slice_w : 2 * slice_w].astype(BF), last.astype(BF)],
        axis=0,
    )
    moved = dot(bits(jnp.logical_or(chosen, carried)), data).astype(BF)
    send_ref[...] = moved.reshape(send_ref.shape)

    lane = iota((col_n, 128), 1)
    dec = jnp.zeros((col_n, 128), F32)
    for k in range(2):
        own = (2 * b + k).astype(F32)
        got = jnp.zeros((col_n, 1), F32)
        for j in range(top):
            hit = meta[:, 16 + j : 17 + j] == own
            got = jnp.where(hit, meta[:, 16 + top + j : 17 + top + j], got)
        dec = jnp.where(lane == k, got, dec)
    even = bits(iota((col_n // 2, col_n), 1) == 2 * iota((col_n // 2, col_n), 0))
    decw_ref[...] = dot(even, dec.astype(BF))


def head_kernel(got_ref, val_ref, proj_ref, res_ref, send_ref):
    r = lax.axis_index("req")
    b = lax.axis_index("blk")
    n_src, block, slice_w = got_ref.shape
    n_dst, n_out, _ = send_ref.shape
    n_slot = n_out - 8
    half = n_slot // 2
    got = got_ref[...].reshape(n_src * block, slice_w)
    column, place, second, slot = slot_of(iota((n_slot, n_src * block), 1))
    target = second * half + column * CAP + slot
    keep = jnp.logical_and(iota((n_slot, n_src * block), 0) == target, place < 2 * CAP)
    slots = dot(bits(keep), got).astype(BF)
    for d in range(n_dst):
        send_ref[d, :n_slot, :] = slots

    line = iota((3 * n_src, n_src * block), 0)
    part = iota((3 * n_src, n_src * block), 1) == (line & (n_src - 1)) * block + 12 + (line >> 5)
    part = dot(bits(part), got)
    stats = part[2 * n_src :]
    peak = stats[:, 0:1] + stats[:, 1:2] + stats[:, 2:3]
    total = stats[:, 3:4] + stats[:, 4:5] + stats[:, 5:6]
    share = total * jnp.exp(peak - jnp.max(peak, axis=0, keepdims=True))
    whole = jnp.sum(share, axis=0, keepdims=True)
    low = jnp.sum(part[:n_src] * share, axis=0, keepdims=True) / whole
    high = jnp.sum(part[n_src : 2 * n_src] * share, axis=0, keepdims=True) / whole
    o_latent = jnp.broadcast_to(jnp.concatenate([low, high], axis=1), (8, 2 * slice_w)).astype(BF)
    head = b & 1
    request = b >> 1
    head_value = dot(o_latent, val_ref[head]).astype(BF)
    projected = dot(head_value, proj_ref[head])[0:1]
    resid = res_ref[...].astype(F32)
    resid = jnp.where(iota(resid.shape, 0) == (request & 1), resid, 0.0)
    resid = jnp.sum(resid, axis=0, keepdims=True)
    owner = jnp.logical_and(request >> 1 == r, head == 0)
    projected = projected + jnp.where(owner, resid, 0.0)
    folded = jnp.concatenate(
        [projected[:, slice_w * j : slice_w * (j + 1)] for j in range(8)], axis=0
    ).astype(BF)
    for d in range(n_dst):
        send_ref[d, n_slot:, :] = folded


def sum_kernel(got_ref, send_ref):
    n_src, n_all, _ = got_ref.shape
    total = got_ref[0, n_all - 8 :, :].astype(F32)
    for s in range(1, n_src):
        total = total + got_ref[s, n_all - 8 :, :].astype(F32)
    total = total.astype(BF)
    for d in range(send_ref.shape[0]):
        send_ref[d] = total


def terms_kernel(
    got_ref,
    rows_ref,
    cols_ref,
    gain_ref,
    decw_ref,
    gate_ref,
    up_ref,
    down_ref,
    sg_ref,
    su_ref,
    sd_ref,
    out_ref,
    shared_ref,
    hid_ref,
):
    b = lax.axis_index("blk")
    n_src, fold, slice_w = got_ref.shape
    dec_n = n_src // 2
    n_line = fold * dec_n
    got = got_ref[...].reshape(n_src * fold, slice_w)
    line = iota((n_line, n_src * fold), 0)
    col = iota((n_line, n_src * fold), 1)
    pick = jnp.logical_and(col >> 4 == (line & (dec_n - 1)), (col & 7) == line >> 4)
    hidden = dot(bits(pick), got).astype(BF)
    wide = hidden.astype(F32)
    chunks = [wide[j * dec_n : (j + 1) * dec_n] for j in range(fold)]
    square = sum(jnp.sum(c * c, axis=1, keepdims=True) for c in chunks)
    factor = lax.rsqrt(square / (fold * slice_w) + 1e-06)
    normed = [
        (c * factor * gain_ref[:, j * slice_w : (j + 1) * slice_w]).astype(BF)
        for j, c in enumerate(chunks)
    ]

    col_n = cols_ref.shape[0]
    x = jnp.concatenate([cols_ref[...], jnp.concatenate(normed, axis=1)], axis=0)
    act = silu_mul(dot_t(x, sg_ref[...]), dot_t(x, su_ref[...]))
    shared = dot(act, sd_ref[...])
    shared_ref[...] = shared[:col_n].astype(BF)
    mine = jnp.where(iota((dec_n, 1), 0) == (b >> 1), 1.0, 0.0) * jnp.where((b & 1) == 0, 1.0, 0.0)
    dec = [mine * shared[col_n:, j * slice_w : (j + 1) * slice_w] for j in range(fold)]

    n_dst, n_row, _ = out_ref.shape
    half = (n_row - 16) // 2
    for k in range(gate_ref.shape[0]):
        span = pl.ds(k * half, half)
        gate, up = 0.0, 0.0
        for s in range(n_dst):
            x = jnp.concatenate([rows_ref[s, span, :], normed[s]], axis=0)
            lanes = slice(s * slice_w, (s + 1) * slice_w)
            gate = gate + dot_t(x, gate_ref[k, :, lanes])
            up = up + dot_t(x, up_ref[k, :, lanes])
        act = silu_mul(gate, up)
        for d in range(n_dst):
            out = dot(act, down_ref[k, :, d * slice_w : (d + 1) * slice_w])
            out_ref[d, span, :] = out[:half].astype(BF)
            dec[d] = dec[d] + decw_ref[:, k : k + 1] * out[half:]

    line = iota((n_line, n_line), 0)
    col = iota((n_line, n_line), 1)
    swap = bits(col == (line & 7) * dec_n + (line >> 3))
    turned = dot(swap, jnp.concatenate([d.astype(BF) for d in dec], axis=0)).astype(BF)
    out_ref[:, n_row - 16 :, :] = turned.reshape(n_dst, 16, slice_w)
    hid_ref[...] = dot(swap, hidden).astype(BF).reshape(hid_ref.shape)


def return_kernel(got_ref, send_ref):
    n_src, n_all, slice_w = got_ref.shape
    n_dst = send_ref.shape[0]
    n_slot = n_all - 16
    half = n_slot // 2
    total = got_ref[0].astype(F32)
    for s in range(1, n_src):
        total = total + got_ref[s].astype(F32)
    total = total.astype(BF)
    column, place, second, slot = slot_of(iota((n_dst * 16, n_slot), 0))
    source = second * half + column * CAP + slot
    keep = jnp.logical_and(iota((n_dst * 16, n_slot), 1) == source, place < 2 * CAP)
    send_ref[:, :16, :] = dot(bits(keep), total[:n_slot]).astype(BF).reshape(n_dst, 16, slice_w)
    dec = total[n_slot:]
    for d in range(n_dst):
        send_ref[d, 16:, :] = dec


def combine_kernel(got_ref, comb_ref, shared_ref, hid_ref, send_ref, dec_ref):
    r = lax.axis_index("req")
    n_src, _, slice_w = got_ref.shape
    n_dst, pre_n, _ = send_ref.shape
    col_n = n_dst * pre_n
    slots = got_ref[:, :16, :].reshape(n_src * 16, slice_w)
    total = lax.dot_general(comb_ref[...], slots, (((0,), (0,)), ((), ())), preferred_element_type=F32)
    total = total[:col_n]
    first = rounded(total)
    shared = shared_ref[...].astype(F32)
    for d in range(n_dst):
        rows = slice(d * pre_n, (d + 1) * pre_n)
        send_ref[d] = jnp.concatenate(
            [first[rows], total[rows] - first[rows], shared[rows]], axis=1
        ).astype(BF)
    dec = hid_ref[r].astype(F32)
    moe = got_ref[0, 16:, :].astype(F32)
    for s in range(1, n_src):
        moe = moe + got_ref[s, 16:, :].astype(F32)
    dec = dec + moe
    dec_ref[...] = jnp.concatenate(
        [
            jnp.concatenate([dec[8 * i + j : 8 * i + j + 1] for j in range(8)], axis=1)
            for i in range(2)
        ],
        axis=0,
    ).astype(BF)


def finish_kernel(got_ref, res_ref, out_ref):
    n_src = got_ref.shape[0]
    slice_w = out_ref.shape[1] // n_src
    got = [got_ref[s].astype(F32) for s in range(n_src)]
    total = jnp.concatenate([g[:, :slice_w] + g[:, slice_w : 2 * slice_w] for g in got], axis=1)
    for g in got:
        total = total + g[:, 2 * slice_w :]
    out_ref[...] = (res_ref[...].astype(F32) + total).astype(BF)


def call(kernel, outs, args, flops, moved, specs=None, scratch=()):
    return pl.pallas_call(
        kernel,
        out_shape=outs,
        in_specs=specs or [VMEM] * len(args),
        out_specs=jax.tree.map(lambda _: VMEM, outs),
        scratch_shapes=scratch,
        cost_estimate=pl.CostEstimate(flops=flops, bytes_accessed=moved, transcendentals=0),
        compiler_params=pltpu.CompilerParams(vmem_limit_bytes=16 << 20),
    )(*args)


def local(
    prefill_resid,
    prefill_routes,
    prefill_scores,
    decode_resid,
    queries,
    latent_cache,
    new_latent,
    cache_lengths,
    decode_routes,
    decode_scores,
    norm_gain,
    absorb_key,
    absorb_value,
    out_proj,
    expert_gate,
    expert_up,
    expert_down,
    shared_gate,
    shared_up,
    shared_down,
):
    req_n = lax.axis_size("req")
    blk_n = lax.axis_size("blk")
    pre_n, width = prefill_resid.shape
    slice_w = width // req_n
    col_n = pre_n * req_n
    part_w = absorb_key.shape[2] + 128
    n_slot = 2 * CAP * blk_n
    gain = norm_gain[None]

    def shape(*dims, dtype=BF):
        return jax.ShapeDtypeStruct(dims, dtype)

    with jax.named_scope("start"):
        sources = (
            queries,
            absorb_key,
            prefill_resid,
            gain,
            prefill_routes,
            prefill_scores,
            decode_routes,
            decode_scores,
            new_latent,
            cache_lengths,
            jnp.swapaxes(latent_cache, 1, 2),
        )
        held = [pltpu.VMEM(a.shape, a.dtype) for a in sources]
        held[9] = pltpu.SMEM(cache_lengths.shape, cache_lengths.dtype)
        sent = call(
            start_kernel,
            shape(req_n, pre_n, width + 128 + part_w),
            tuple(pltpu.with_memory_space_constraint(a, pltpu.HBM) for a in sources),
            10**8,
            4 * 10**6,
            specs=[pl.BlockSpec(memory_space=pltpu.HBM)] * len(sources),
            scratch=held + [pltpu.SemaphoreType.DMA((len(sources),))],
        )
        got = exchange(sent, "req")
    with jax.named_scope("route"):
        sent, cols, comb, decw = call(
            route_kernel,
            (
                shape(blk_n, 16, slice_w),
                shape(col_n, width),
                shape(blk_n * 16, 128),
                shape(16, 128, dtype=F32),
            ),
            (got,),
            10**7,
            10**6,
        )
        got = exchange(sent, "blk")
    with jax.named_scope("heads"):
        sent = call(
            head_kernel,
            shape(req_n, n_slot + 8, slice_w),
            (got, absorb_value, out_proj, decode_resid),
            10**8,
            3 * 10**6,
        )
        rows = exchange(sent, "req")
    with jax.named_scope("hidden"):
        sent = call(sum_kernel, shape(blk_n, 8, slice_w), (rows,), 10**5, 3 * 10**5)
        got = exchange(sent, "blk")
    with jax.named_scope("experts"):
        sent, shared, hidden = call(
            terms_kernel,
            (
                shape(req_n, n_slot + 16, slice_w),
                shape(col_n, width),
                shape(req_n, 16, slice_w),
            ),
            (
                got,
                rows,
                cols,
                gain,
                decw,
                jnp.swapaxes(expert_gate, 1, 2),
                jnp.swapaxes(expert_up, 1, 2),
                expert_down,
                shared_gate.T,
                shared_up.T,
                shared_down,
            ),
            8 * 10**9,
            12 * 10**6,
        )
        got = exchange(sent, "req")
    with jax.named_scope("return"):
        sent = call(return_kernel, shape(blk_n, 32, slice_w), (got,), 10**8, 3 * 10**6)
        got = exchange(sent, "blk")
    with jax.named_scope("combine"):
        sent, decode_out = call(
            combine_kernel,
            (shape(req_n, pre_n, 2 * slice_w + width), shape(2, width)),
            (got, comb, shared, hidden),
            10**7,
            10**6,
        )
        got = exchange(sent, "req")
    with jax.named_scope("finish"):
        prefill_out = call(finish_kernel, shape(pre_n, width), (got, prefill_resid), 10**5, 10**5)
    return (prefill_out, decode_out)


def solution(mesh):
    return jax.shard_map(
        local,
        mesh=mesh,
        in_specs=(
            P(("blk", "req"), None),
            P(("blk", "req"), None),
            P(("blk", "req"), None),
            P("req", None),
            P("req", None, None),
            P("req", "blk", None),
            P("req", None),
            P("req"),
            P("req", None),
            P("req", None),
            P(),
            P(),
            P("req", None, None),
            P("req", None, None),
            P("blk", None, "req"),
            P("blk", None, "req"),
            P("blk", "req", None),
            P(None, "req"),
            P(None, "req"),
            P("req", None),
        ),
        out_specs=(P(("blk", "req"), None), P("req", None)),
        check_vma=False,
    )
```

time: 1080 us -> 145 us (0.13)
  waiting for transfers between devices: 544 us -> 0 us
  blocking collectives: 371 us -> 134 us
  matrix products: 57.8 us -> 0 us
  local copies, waits for them, and re-layouts: 50.5 us -> 0.06 us
  other arithmetic: 36.9 us -> 0 us
  between operations: 14.8 us -> 0.77 us
    all_gather x3 -> x0, blocking collectives: 371 us -> none  [the longest x1 306 us: local(): lax.all_gather(own_table, ('req', 'blk'), axis=0, tiled=True)]
    unnamed x6 -> x0, waiting for transfers between devices: 286 us -> none
    all_gather x4 -> x0, waiting for transfers between devices: 258 us -> none  [the longest x1 115 us: local(): proj_piece = lax.all_gather(out_proj, 'req', axis=0, tiled=True)]
    all_to_all x0 -> x7, blocking collectives: none -> 134 us  [exchange(): return lax.all_to_all(payload, axis, 0, 0, tiled=True)]
    dot_general x12 -> x0, matrix products: 57.8 us -> none  [the longest x3 31.7 us: swiglu(): return jnp.dot(hidden, down_w, preferred_element_type=jnp.float32)]
    add x64 -> x0, other arithmetic: 29.4 us -> none  [the longest x31 28.6 us: merge_parts(): first_part[2] * keep_first[:, :, None]]
    dot_general x1 -> x0, local copies, waits for them, and re-layouts: 17.8 us -> none  [local(): jnp.einsum('tr,rnd->tnd', selector, shared_column, precision=lax.Precisio...]
    reshape x3 -> x0, local copies, waits for them, and re-layouts: 16 us -> none  [the longest x1 15.9 us: local(): shared_part.reshape(tile_rows * lax.axis_size(('req', 'blk')), model_width)]
  transfers between devices with their start and end apart: 5 -> 0, of which waited for: 5 -> 0; matrix products, arithmetic and copies ran while one was open for 3% -> 0% of each run, Pallas kernels for 0% -> 0%
where the time goes in v2:
time: 145 us
  blocking collectives  134 us (92%)
  Pallas kernels  9.66 us (7%)
    all_to_all x7, blocking collectives, exchange(): return lax.all_to_all(payload, axis, 0, 0, tiled=True)  134 us
    pallas_call x8, Pallas kernels, call(): pl.pallas_call(kernel, out_shape=outs, in_specs=specs or [VMEM] * len(arg...  9.66 us

profile of v2, /device:TPU:2, one launch (start us, length us, event | category | flops | bytes accessed | tf_op | source)
XLA Modules:
  0.0 144.9 jit_solution(9739416005893958805)
XLA Ops:
  0.6 0.0 copy-start
  0.6 0.0 copy-start.1
  0.7 0.0 copy-start.3
  0.7 3.1 %start.1 = bf16[8,4,2816]{2,1,0:T(4,128)(2,1)S(1)} custom-call(bf16[2,16,192]{2,1,0:T(8,128)(2,1)} %refs_0_.1, bf16[16,128,512]{2,1,0:T(8,128)(2,1)} %refs_1_.1, bf16[4,2048]{1,0:T(4,128)(2,1)} %res_ref.3, f32[1,2048]{1,0:T(1,128)} %bitcast.6, s32[4,6]{1,0:T(4,128)} %refs_4_.1, f32[4,6]{1,0:T(4,128)} %refs_5_.1, s32[2,6]{1,0:T(2,128)} %refs_6_.1, ...), custom_call_target="tpu_custom_call" | custom-call | flops 100000000 | bytes 4000000 | tf_op jit(solution)/shard_map/start/pallas_call | solution.py:376
  3.8 14.4 %all_to_all.35.got_ref = bf16[8,4,2816]{2,1,0:T(4,128)(2,1)S(1)} all-to-all(bf16[8,4,2816]{2,1,0:T(4,128)(2,1)S(1)} %start.1), channel_id=1, replica_groups=mesh['req'=8,'blk'=32] {'req'}, dimensions={0} | all-to-all | bytes 360448 | tf_op jit(solution)/shard_map/start/all_to_all | solution.py:19
  18.2 0.7 route.1
  18.9 0.0 copy-start.10
  18.9 22.1 %all_to_all.36.got_ref = bf16[32,16,256]{2,1,0:T(8,128)(2,1)S(1)} all-to-all(bf16[32,16,256]{2,1,0:T(8,128)(2,1)S(1)} %get-tuple-element.11), channel_id=1, replica_groups=mesh['req'=8,'blk'=32] {'blk'}, dimensions={0} | all-to-all | bytes 524288 | tf_op jit(solution)/shard_map/route/all_to_all | solution.py:19
  41.0 0.0 copy-done
  41.0 0.0 copy-done.1
  41.0 0.0 copy-done.3
  41.0 0.0 copy-start.8
  41.0 0.0 copy-start.9
  41.0 0.8 heads.1
  41.8 0.0 copy-start.6
  41.8 0.0 copy-start.7
  41.8 25.8 %all_to_all.37.got_ref.rows_ref = bf16[8,392,256]{2,1,0:T(8,128)(2,1)S(1)} all-to-all(bf16[8,392,256]{2,1,0:T(8,128)(2,1)S(1)} %heads.1), channel_id=1, replica_groups=mesh['req'=8,'blk'=32] {'req'}, dimensions={0} | all-to-all | bytes 3211264 | tf_op jit(solution)/shard_map/heads/all_to_all | solution.py:19
  67.6 0.0 copy-start.4
  67.6 0.0 copy-start.5
  67.6 13.6 %all_to_all.38.got_ref = bf16[32,8,256]{2,1,0:T(8,128)(2,1)S(1)} all-to-all(bf16[32,8,256]{2,1,0:T(8,128)(2,1)S(1)} %hidden.1), channel_id=1, replica_groups=mesh['req'=8,'blk'=32] {'blk'}, dimensions={0} | all-to-all | bytes 262144 | tf_op jit(solution)/shard_map/hidden/all_to_all | solution.py:19
  81.2 0.0 copy-done.10
  81.2 0.0 copy-done.8
  81.2 0.0 copy-done.9
  81.2 0.0 copy-done.6
  81.3 0.0 copy-done.7
  81.3 0.0 copy-done.4
  81.3 0.0 copy-done.5
  81.3 3.2 %experts.1 = (bf16[8,400,256]{2,1,0:T(8,128)(2,1)S(1)}, bf16[32,2048]{1,0:T(8,128)(2,1)S(1)}, bf16[8,16,256]{2,1,0:T(8,128)(2,1)S(1)}) custom-call(bf16[32,8,256]{2,1,0:T(8,128)(2,1)S(1)} %all_to_all.38.got_ref, bf16[8,392,256]{2,1,0:T(8,128)(2,1)S(1)} %all_to_all.37.got_ref.rows_ref, bf16[32,2048]{1,0:T(8,128)(2,1)S(1)} %get-tuple-element.12.cols_ref, ...), custom_call_target="tpu_custom_call" | custom-call | flops 8000000000 | bytes 12000000 | tf_op jit(solution)/shard_map/experts/pallas_call | solution.py:376
  84.5 25.5 %all_to_all.39.got_ref = bf16[8,400,256]{2,1,0:T(8,128)(2,1)S(1)} all-to-all(bf16[8,400,256]{2,1,0:T(8,128)(2,1)S(1)} %get-tuple-element.14), channel_id=1, replica_groups=mesh['req'=8,'blk'=32] {'req'}, dimensions={0} | all-to-all | bytes 3276800 | tf_op jit(solution)/shard_map/experts/all_to_all | solution.py:19
  110.0 0.5 return.1
  110.4 0.0 copy-start.2
  110.5 21.8 %all_to_all.40.got_ref = bf16[32,32,256]{2,1,0:T(8,128)(2,1)S(1)} all-to-all(bf16[32,32,256]{2,1,0:T(8,128)(2,1)S(1)} %return.1), channel_id=1, replica_groups=mesh['req'=8,'blk'=32] {'blk'}, dimensions={0} | all-to-all | bytes 1048576 | tf_op jit(solution)/shard_map/return/all_to_all | solution.py:19
  132.2 0.8 combine.1
  133.0 11.2 %all_to_all.41.got_ref = bf16[8,4,2560]{2,1,0:T(4,128)(2,1)S(1)} all-to-all(bf16[8,4,2560]{2,1,0:T(4,128)(2,1)S(1)} %get-tuple-element.18), channel_id=1, replica_groups=mesh['req'=8,'blk'=32] {'req'}, dimensions={0} | all-to-all | bytes 327680 | tf_op jit(solution)/shard_map/combine/all_to_all | solution.py:19
  144.2 0.0 copy-done.2
  144.2 0.7 finish.1
  (1 shorter events, 0.0 us)
Async XLA Ops:
  0.6 40.3 %copy-start = (bf16[2,128,2048]{2,1,0:T(8,128)(2,1)S(1)}, bf16[2,128,2048]{2,1,0:T(8,128)(2,1)}, u32[]{:S(2)}) copy-start(bf16[2,128,2048]{2,1,0:T(8,128)(2,1)} %proj_ref.1) | copy-start | bytes 3145732
  0.6 40.3 %copy-start.1 = (bf16[2,512,128]{2,1,0:T(8,128)(2,1)S(1)}, bf16[2,512,128]{2,1,0:T(8,128)(2,1)}, u32[]{:S(2)}) copy-start(bf16[2,512,128]{2,1,0:T(8,128)(2,1)} %val_ref.1) | copy-start | bytes 786436
  0.7 40.3 %copy-start.3 = (bf16[2,2048]{1,0:T(2,128)(2,1)S(1)}, bf16[2,2048]{1,0:T(2,128)(2,1)}, u32[]{:S(2)}) copy-start(bf16[2,2048]{1,0:T(2,128)(2,1)} %res_ref.2) | copy-start | bytes 24580
  18.9 62.4 %copy-start.10 = (bf16[352,2048]{1,0:T(8,128)(2,1)S(1)}, bf16[352,2048]{1,0:T(8,128)(2,1)}, u32[]{:S(2)}) copy-start(bf16[352,2048]{1,0:T(8,128)(2,1)} %sd_ref.1) | copy-start | bytes 4325380
  41.0 40.3 %copy-start.8 = (bf16[2048,352]{0,1:T(8,128)(2,1)S(1)}, bf16[2048,352]{0,1:T(8,128)(2,1)}, u32[]{:S(2)}) copy-start(bf16[2048,352]{0,1:T(8,128)(2,1)} %param.37) | copy-start | bytes 4325380
  41.0 40.3 %copy-start.9 = (bf16[2048,352]{0,1:T(8,128)(2,1)S(1)}, bf16[2048,352]{0,1:T(8,128)(2,1)}, u32[]{:S(2)}) copy-start(bf16[2048,352]{0,1:T(8,128)(2,1)} %param.38) | copy-start | bytes 4325380
  41.8 39.5 %copy-start.6 = (bf16[2,2048,176]{1,2,0:T(8,128)(2,1)S(1)}, bf16[2,2048,176]{1,2,0:T(8,128)(2,1)}, u32[]{:S(2)}) copy-start(bf16[2,2048,176]{1,2,0:T(8,128)(2,1)} %param.35) | copy-start | bytes 4325380
  41.8 39.5 %copy-start.7 = (bf16[2,176,2048]{2,1,0:T(8,128)(2,1)S(1)}, bf16[2,176,2048]{2,1,0:T(8,128)(2,1)}, u32[]{:S(2)}) copy-start(bf16[2,176,2048]{2,1,0:T(8,128)(2,1)} %down_ref.1) | copy-start | bytes 4325380
  67.6 13.7 %copy-start.4 = (f32[2048]{0:T(1024)S(1)}, f32[2048]{0:T(1024)}, u32[]{:S(2)}) copy-start(f32[2048]{0:T(1024)} %param.30) | copy-start | bytes 24580
  67.6 13.7 %copy-start.5 = (bf16[2,2048,176]{1,2,0:T(8,128)(2,1)S(1)}, bf16[2,2048,176]{1,2,0:T(8,128)(2,1)}, u32[]{:S(2)}) copy-start(bf16[2,2048,176]{1,2,0:T(8,128)(2,1)} %param.34) | copy-start | bytes 4325380
  110.4 33.8 %copy-start.2 = (bf16[4,2048]{1,0:T(4,128)(2,1)S(1)}, bf16[4,2048]{1,0:T(4,128)(2,1)}, u32[]{:S(2)}) copy-start(bf16[4,2048]{1,0:T(4,128)(2,1)} %res_ref.3) | copy-start | bytes 49156

commit v3 on v2

--- a/solution.py
+++ b/solution.py
@@ -312,33 +312,48 @@
     swap = bits(col == (line & 7) * dec_n + (line >> 3))
     turned = dot(swap, jnp.concatenate([d.astype(BF) for d in dec], axis=0)).astype(BF)
     out_ref[:, n_row - 16 :, :] = turned.reshape(n_dst, 16, slice_w)
-    hid_ref[...] = dot(swap, hidden).astype(BF).reshape(hid_ref.shape)
-
-
-def return_kernel(got_ref, send_ref):
-    n_src, n_all, slice_w = got_ref.shape
-    n_dst = send_ref.shape[0]
-    n_slot = n_all - 16
-    half = n_slot // 2
+    hid_ref[...] = dot(swap, hidden).reshape(hid_ref.shape).astype(BF)
+
+
+def hidden_sum_kernel(got_ref, slots_ref, keep_ref, give_ref):
+    b = lax.axis_index("blk")
+    n_src = got_ref.shape[0]
+    n_slot = slots_ref.shape[0]
     total = got_ref[0].astype(F32)
     for s in range(1, n_src):
         total = total + got_ref[s].astype(F32)
-    total = total.astype(BF)
-    column, place, second, slot = slot_of(iota((n_dst * 16, n_slot), 0))
-    source = second * half + column * CAP + slot
-    keep = jnp.logical_and(iota((n_dst * 16, n_slot), 1) == source, place < 2 * CAP)
-    send_ref[:, :16, :] = dot(bits(keep), total[:n_slot]).astype(BF).reshape(n_dst, 16, slice_w)
+    slots_ref[...] = total[:n_slot].astype(BF)
     dec = total[n_slot:]
-    for d in range(n_dst):
-        send_ref[d, 16:, :] = dec
+    low = jnp.concatenate([dec[0:4], dec[8:12]], axis=0)
+    high = jnp.concatenate([dec[4:8], dec[12:16]], axis=0)
+    even = (b & 1) == 0
+    keep_ref[...] = jnp.where(even, low, high)
+    give_ref[...] = jnp.where(even, high, low).astype(BF)
+
+
+def return_kernel(slots_ref, keep_ref, other_ref, send_ref):
+    n_slot = slots_ref.shape[0]
+    n_dst, block, _ = send_ref.shape
+    half = n_slot // 2
+    dec = (keep_ref[...] + other_ref[...].astype(F32)).astype(BF)
+    data = jnp.concatenate([slots_ref[...], dec, jnp.zeros_like(dec)], axis=0)
+    column, place, second, slot = slot_of(iota((n_dst * block, n_slot + 16), 0))
+    col = iota((n_dst * block, n_slot + 16), 1)
+    source = jnp.where(
+        place < 2 * CAP,
+        second * half + column * CAP + slot,
+        n_slot + 4 * (column & 1) + place - 2 * CAP,
+    )
+    send_ref[...] = dot(bits(col == source), data).astype(BF).reshape(send_ref.shape)
 
 
 def combine_kernel(got_ref, comb_ref, shared_ref, hid_ref, send_ref, dec_ref):
     r = lax.axis_index("req")
+    b = lax.axis_index("blk")
     n_src, _, slice_w = got_ref.shape
     n_dst, pre_n, _ = send_ref.shape
     col_n = n_dst * pre_n
-    slots = got_ref[:, :16, :].reshape(n_src * 16, slice_w)
+    slots = got_ref[...].reshape(n_src * 16, slice_w)
     total = lax.dot_general(comb_ref[...], slots, (((0,), (0,)), ((), ())), preferred_element_type=F32)
     total = total[:col_n]
     first = rounded(total)
@@ -348,21 +363,15 @@
         send_ref[d] = jnp.concatenate(
             [first[rows], total[rows] - first[rows], shared[rows]], axis=1
         ).astype(BF)
-    dec = hid_ref[r].astype(F32)
-    moe = got_ref[0, 16:, :].astype(F32)
-    for s in range(1, n_src):
-        moe = moe + got_ref[s, 16:, :].astype(F32)
-    dec = dec + moe
-    dec_ref[...] = jnp.concatenate(
-        [
-            jnp.concatenate([dec[8 * i + j : 8 * i + j + 1] for j in range(8)], axis=1)
-            for i in range(2)
-        ],
-        axis=0,
-    ).astype(BF)
-
-
-def finish_kernel(got_ref, res_ref, out_ref):
+    line = iota((8, n_src * 16), 0)
+    col = iota((8, n_src * 16), 1)
+    pick = jnp.logical_and((col & 15) == 12 + (line & 3), ((col >> 4) & 1) == line >> 2)
+    moe = dot(bits(pick), slots)
+    dec_ref[...] = (hid_ref[2 * r + (b & 1)].astype(F32) + moe).astype(BF)
+
+
+def finish_kernel(got_ref, res_ref, own_ref, other_ref, out_ref, dec_ref):
+    b = lax.axis_index("blk")
     n_src = got_ref.shape[0]
     slice_w = out_ref.shape[1] // n_src
     got = [got_ref[s].astype(F32) for s in range(n_src)]
@@ -370,6 +379,16 @@
     for g in got:
         total = total + g[:, 2 * slice_w :]
     out_ref[...] = (res_ref[...].astype(F32) + total).astype(BF)
+
+    def flat(ref):
+        folded = ref[...].astype(F32)
+        return jnp.concatenate([folded[j : j + 1] for j in range(n_src)], axis=1)
+
+    own, other = flat(own_ref), flat(other_ref)
+    even = (b & 1) == 0
+    dec_ref[...] = jnp.concatenate(
+        [jnp.where(even, own, other), jnp.where(even, other, own)], axis=0
+    ).astype(BF)
 
 
 def call(kernel, outs, args, flops, moved, specs=None, scratch=()):
@@ -414,6 +433,7 @@
     part_w = absorb_key.shape[2] + 128
     n_slot = 2 * CAP * blk_n
     gain = norm_gain[None]
+    sibling = [(i, i ^ 1) for i in range(blk_n)]
 
     def shape(*dims, dtype=BF):
         return jax.ShapeDtypeStruct(dims, dtype)
@@ -476,7 +496,7 @@
             (
                 shape(req_n, n_slot + 16, slice_w),
                 shape(col_n, width),
-                shape(req_n, 16, slice_w),
+                shape(2 * req_n, 8, slice_w),
             ),
             (
                 got,
@@ -496,19 +516,34 @@
         )
         got = exchange(sent, "req")
     with jax.named_scope("return"):
-        sent = call(return_kernel, shape(blk_n, 32, slice_w), (got,), 10**8, 3 * 10**6)
+        slots, keep, give = call(
+            hidden_sum_kernel,
+            (shape(n_slot, slice_w), shape(8, slice_w, dtype=F32), shape(8, slice_w)),
+            (got,),
+            10**6,
+            2 * 10**6,
+        )
+        other = lax.ppermute(give, "blk", sibling)
+        sent = call(return_kernel, shape(blk_n, 16, slice_w), (slots, keep, other), 10**8, 10**6)
         got = exchange(sent, "blk")
     with jax.named_scope("combine"):
-        sent, decode_out = call(
+        sent, own_row = call(
             combine_kernel,
-            (shape(req_n, pre_n, 2 * slice_w + width), shape(2, width)),
+            (shape(req_n, pre_n, 2 * slice_w + width), shape(8, slice_w)),
             (got, comb, shared, hidden),
             10**7,
             10**6,
         )
+        other_row = lax.ppermute(own_row, "blk", sibling)
         got = exchange(sent, "req")
     with jax.named_scope("finish"):
-        prefill_out = call(finish_kernel, shape(pre_n, width), (got, prefill_resid), 10**5, 10**5)
+        prefill_out, decode_out = call(
+            finish_kernel,
+            (shape(pre_n, width), shape(2, width)),
+            (got, prefill_resid, own_row, other_row),
+            10**5,
+            10**5,
+        )
     return (prefill_out, decode_out)
 
 

time: 145 us -> 142 us (0.979)
  blocking collectives: 134 us -> 118 us
  waiting for transfers between devices: 0 us -> 8.28 us
  starting transfers between devices: 0 us -> 4.62 us
    all_to_all x7 -> x6, blocking collectives: 134 us -> 118 us  [exchange(): return lax.all_to_all(payload, axis, 0, 0, tiled=True)]
    all_to_all x0 -> x1, waiting for transfers between devices: none -> 5.97 us  [exchange(): return lax.all_to_all(payload, axis, 0, 0, tiled=True)]
    all_to_all x0 -> x1, starting transfers between devices: none -> 4.53 us  [exchange(): return lax.all_to_all(payload, axis, 0, 0, tiled=True)]
    ppermute x0 -> x2, waiting for transfers between devices: none -> 2.32 us  [the longest x1 1.16 us: local(): other_row = lax.ppermute(own_row, 'blk', sibling)]
    pallas_call x8 -> x9, Pallas kernels: 9.66 us -> 9.84 us  [call(): pl.pallas_call(kernel, out_shape=outs, in_specs=specs or [VMEM] * len(arg...]
  transfers between devices with their start and end apart: 0 -> 3, of which waited for: 0 -> 3; matrix products, arithmetic and copies ran while one was open for 0% -> 0% of each run, Pallas kernels for 0% -> 0%
where the time goes in v3:
time: 142 us; the launch traced here: 141 us
  blocking collectives  118 us (83%)
  Pallas kernels  9.84 us (7%)
  waiting for transfers between devices  8.28 us (6%)
  starting transfers between devices  4.62 us (3%)
    all_to_all x6, blocking collectives, exchange(): return lax.all_to_all(payload, axis, 0, 0, tiled=True)  118 us
    pallas_call x9, Pallas kernels, call(): pl.pallas_call(kernel, out_shape=outs, in_specs=specs or [VMEM] * len(arg...  9.84 us
    all_to_all x1, waiting for transfers between devices, exchange(): return lax.all_to_all(payload, axis, 0, 0, tiled=True)  5.97 us
    all_to_all x1, starting transfers between devices, exchange(): return lax.all_to_all(payload, axis, 0, 0, tiled=True)  4.53 us
  transfers between devices with their start and end apart: 3, of which 3 were waited for; matrix products, arithmetic and copies ran while one was open for 0% of the time, Pallas kernels for 0%

profile of v3, /device:TPU:2, one launch (start us, length us, event | category | flops | bytes accessed | tf_op | source)
XLA Modules:
  0.0 141.5 jit_solution(2032594650436758719)
XLA Ops:
  0.6 0.0 copy-start
  0.6 0.0 copy-start.1
  0.7 0.0 copy-start.3
  0.7 3.1 %start.1 = bf16[8,4,2816]{2,1,0:T(4,128)(2,1)S(1)} custom-call(bf16[2,16,192]{2,1,0:T(8,128)(2,1)} %refs_0_.1, bf16[16,128,512]{2,1,0:T(8,128)(2,1)} %refs_1_.1, bf16[4,2048]{1,0:T(4,128)(2,1)} %res_ref.3, f32[1,2048]{1,0:T(1,128)} %bitcast.6, s32[4,6]{1,0:T(4,128)} %refs_4_.1, f32[4,6]{1,0:T(4,128)} %refs_5_.1, s32[2,6]{1,0:T(2,128)} %refs_6_.1, ...), custom_call_target="tpu_custom_call" | custom-call | flops 100000000 | bytes 4000000 | tf_op jit(solution)/shard_map/start/pallas_call | solution.py:395
  3.8 14.4 %all_to_all.35.got_ref = bf16[8,4,2816]{2,1,0:T(4,128)(2,1)S(1)} all-to-all(bf16[8,4,2816]{2,1,0:T(4,128)(2,1)S(1)} %start.1), channel_id=1, replica_groups=mesh['req'=8,'blk'=32] {'req'}, dimensions={0} | all-to-all | bytes 360448 | tf_op jit(solution)/shard_map/start/all_to_all | solution.py:19
  18.2 0.7 route.1
  18.9 0.0 copy-start.10
  18.9 22.1 %all_to_all.36.got_ref = bf16[32,16,256]{2,1,0:T(8,128)(2,1)S(1)} all-to-all(bf16[32,16,256]{2,1,0:T(8,128)(2,1)S(1)} %get-tuple-element.14), channel_id=1, replica_groups=mesh['req'=8,'blk'=32] {'blk'}, dimensions={0} | all-to-all | bytes 524288 | tf_op jit(solution)/shard_map/route/all_to_all | solution.py:19
  41.0 0.0 copy-done
  41.0 0.0 copy-done.1
  41.0 0.0 copy-done.3
  41.0 0.0 copy-start.8
  41.0 0.0 copy-start.9
  41.0 0.8 heads.1
  41.8 0.0 copy-start.6
  41.8 0.0 copy-start.7
  41.8 25.8 %all_to_all.37.got_ref.rows_ref = bf16[8,392,256]{2,1,0:T(8,128)(2,1)S(1)} all-to-all(bf16[8,392,256]{2,1,0:T(8,128)(2,1)S(1)} %heads.1), channel_id=1, replica_groups=mesh['req'=8,'blk'=32] {'req'}, dimensions={0} | all-to-all | bytes 3211264 | tf_op jit(solution)/shard_map/heads/all_to_all | solution.py:19
  67.6 0.0 copy-start.4
  67.6 0.0 copy-start.5
  67.6 13.6 %all_to_all.38.got_ref = bf16[32,8,256]{2,1,0:T(8,128)(2,1)S(1)} all-to-all(bf16[32,8,256]{2,1,0:T(8,128)(2,1)S(1)} %hidden.1), channel_id=1, replica_groups=mesh['req'=8,'blk'=32] {'blk'}, dimensions={0} | all-to-all | bytes 262144 | tf_op jit(solution)/shard_map/hidden/all_to_all | solution.py:19
  81.2 0.0 copy-done.10
  81.2 0.0 copy-done.8
  81.2 0.0 copy-done.9
  81.2 0.0 copy-done.6
  81.3 0.0 copy-done.7
  81.3 0.0 copy-done.4
  81.3 0.0 copy-done.5
  81.3 3.2 %experts.1 = (bf16[8,400,256]{2,1,0:T(8,128)(2,1)S(1)}, bf16[32,2048]{1,0:T(8,128)(2,1)S(1)}, bf16[16,8,256]{2,1,0:T(8,128)(2,1)S(1)}) custom-call(bf16[32,8,256]{2,1,0:T(8,128)(2,1)S(1)} %all_to_all.38.got_ref, bf16[8,392,256]{2,1,0:T(8,128)(2,1)S(1)} %all_to_all.37.got_ref.rows_ref, bf16[32,2048]{1,0:T(8,128)(2,1)S(1)} %get-tuple-element.15.cols_ref, ...), custom_call_target="tpu_custom_call" | custom-call | flops 8000000000 | bytes 12000000 | tf_op jit(solution)/shard_map/experts/pallas_call | solution.py:395
  84.5 25.5 %all_to_all.39.got_ref = bf16[8,400,256]{2,1,0:T(8,128)(2,1)S(1)} all-to-all(bf16[8,400,256]{2,1,0:T(8,128)(2,1)S(1)} %get-tuple-element.17), channel_id=1, replica_groups=mesh['req'=8,'blk'=32] {'req'}, dimensions={0} | all-to-all | bytes 3276800 | tf_op jit(solution)/shard_map/experts/all_to_all | solution.py:19
  110.0 0.0 copy-start.2
  110.0 0.2 return.2
  110.2 0.1 collective-permute-start
  110.3 1.2 collective-permute-done.other_ref
  111.4 0.3 return.3
  111.7 16.5 %all_to_all.40.got_ref = bf16[32,16,256]{2,1,0:T(8,128)(2,1)S(1)} all-to-all(bf16[32,16,256]{2,1,0:T(8,128)(2,1)S(1)} %return.3), channel_id=1, replica_groups=mesh['req'=8,'blk'=32] {'blk'}, dimensions={0} | all-to-all | bytes 524288 | tf_op jit(solution)/shard_map/return/all_to_all | solution.py:19
  128.2 0.9 combine.1
  129.1 4.5 %all-to-all-start.6 = ((bf16[8,4,2560]{2,1,0:T(4,128)(2,1)}), bf16[8,4,2560]{2,1,0:T(4,128)(2,1)S(1)}, u32[]{:S(2)}, u32[]{:S(2)}) async-start(bf16[8,4,2560]{2,1,0:T(4,128)(2,1)} %get-tuple-element.24), calls=%async_computation.6 | async-start | bytes 327680 | tf_op jit(solution)/shard_map/combine/all_to_all | solution.py:19
  133.6 0.0 collective-permute-start.1
  133.7 1.2 collective-permute-done.1.other_ref
  134.8 6.0 %all-to-all-done.6.got_ref = bf16[8,4,2560]{2,1,0:T(4,128)(2,1)S(1)} async-done(((bf16[8,4,2560]{2,1,0:T(4,128)(2,1)}), bf16[8,4,2560]{2,1,0:T(4,128)(2,1)S(1)}, u32[]{:S(2)}, u32[]{:S(2)}) %all-to-all-start.6) | async-done | bytes 163872 | tf_op jit(solution)/shard_map/combine/all_to_all | solution.py:19
  140.8 0.0 copy-done.2
  140.8 0.7 finish.1
  (1 shorter events, 0.0 us)
Async XLA Ops:
  0.6 40.3 %copy-start = (bf16[2,128,2048]{2,1,0:T(8,128)(2,1)S(1)}, bf16[2,128,2048]{2,1,0:T(8,128)(2,1)}, u32[]{:S(2)}) copy-start(bf16[2,128,2048]{2,1,0:T(8,128)(2,1)} %proj_ref.1) | copy-start | bytes 3145732
  0.6 40.3 %copy-start.1 = (bf16[2,512,128]{2,1,0:T(8,128)(2,1)S(1)}, bf16[2,512,128]{2,1,0:T(8,128)(2,1)}, u32[]{:S(2)}) copy-start(bf16[2,512,128]{2,1,0:T(8,128)(2,1)} %val_ref.1) | copy-start | bytes 786436
  0.7 40.3 %copy-start.3 = (bf16[2,2048]{1,0:T(2,128)(2,1)S(1)}, bf16[2,2048]{1,0:T(2,128)(2,1)}, u32[]{:S(2)}) copy-start(bf16[2,2048]{1,0:T(2,128)(2,1)} %res_ref.2) | copy-start | bytes 24580
  18.9 62.4 %copy-start.10 = (bf16[352,2048]{1,0:T(8,128)(2,1)S(1)}, bf16[352,2048]{1,0:T(8,128)(2,1)}, u32[]{:S(2)}) copy-start(bf16[352,2048]{1,0:T(8,128)(2,1)} %sd_ref.1) | copy-start | bytes 4325380
  41.0 40.3 %copy-start.8 = (bf16[2048,352]{0,1:T(8,128)(2,1)S(1)}, bf16[2048,352]{0,1:T(8,128)(2,1)}, u32[]{:S(2)}) copy-start(bf16[2048,352]{0,1:T(8,128)(2,1)} %param.37) | copy-start | bytes 4325380
  41.0 40.3 %copy-start.9 = (bf16[2048,352]{0,1:T(8,128)(2,1)S(1)}, bf16[2048,352]{0,1:T(8,128)(2,1)}, u32[]{:S(2)}) copy-start(bf16[2048,352]{0,1:T(8,128)(2,1)} %param.38) | copy-start | bytes 4325380
  41.8 39.5 %copy-start.6 = (bf16[2,2048,176]{1,2,0:T(8,128)(2,1)S(1)}, bf16[2,2048,176]{1,2,0:T(8,128)(2,1)}, u32[]{:S(2)}) copy-start(bf16[2,2048,176]{1,2,0:T(8,128)(2,1)} %param.35) | copy-start | bytes 4325380
  41.8 39.5 %copy-start.7 = (bf16[2,176,2048]{2,1,0:T(8,128)(2,1)S(1)}, bf16[2,176,2048]{2,1,0:T(8,128)(2,1)}, u32[]{:S(2)}) copy-start(bf16[2,176,2048]{2,1,0:T(8,128)(2,1)} %down_ref.1) | copy-start | bytes 4325380
  67.6 13.7 %copy-start.4 = (f32[2048]{0:T(1024)S(1)}, f32[2048]{0:T(1024)}, u32[]{:S(2)}) copy-start(f32[2048]{0:T(1024)} %param.30) | copy-start | bytes 24580
  67.6 13.7 %copy-start.5 = (bf16[2,2048,176]{1,2,0:T(8,128)(2,1)S(1)}, bf16[2,2048,176]{1,2,0:T(8,128)(2,1)}, u32[]{:S(2)}) copy-start(bf16[2,2048,176]{1,2,0:T(8,128)(2,1)} %param.34) | copy-start | bytes 4325380
  110.0 30.8 %copy-start.2 = (bf16[4,2048]{1,0:T(4,128)(2,1)S(1)}, bf16[4,2048]{1,0:T(4,128)(2,1)}, u32[]{:S(2)}) copy-start(bf16[4,2048]{1,0:T(4,128)(2,1)} %res_ref.3) | copy-start | bytes 49156
  110.2 1.3 collective-permute-start
  129.1 11.7 %all-to-all-start.6 = ((bf16[8,4,2560]{2,1,0:T(4,128)(2,1)}), bf16[8,4,2560]{2,1,0:T(4,128)(2,1)S(1)}, u32[]{:S(2)}, u32[]{:S(2)}) async-start(bf16[8,4,2560]{2,1,0:T(4,128)(2,1)} %get-tuple-element.24), calls=%async_computation.6 | async-start | bytes 327680 | tf_op jit(solution)/shard_map/combine/all_to_all | solution.py:19
  133.6 1.2 collective-permute-start.1

commit v4 on v3

--- a/solution.py
+++ b/solution.py
@@ -8,6 +8,8 @@
 NEG = -1e30
 ROUTE_SCALE = 2.446
 CAP = 6
+HEAD = 16
+SLACK = 48
 BF = jnp.bfloat16
 F32 = jnp.float32
 I32 = jnp.int32
@@ -176,7 +178,14 @@
     comb_ref[...] = jnp.where(chosen, weight, 0.0).astype(BF)
     carried = jnp.logical_and(lane >= col_n, row == (lane & (col_n - 1)) * 16 + 11 + (lane >> 5))
     mine = cols_ref[:, pl.ds(pl.multiple_of(r * slice_w, slice_w), slice_w)]
-    last = jnp.concatenate([pairs[:, 2 * slice_w :], jnp.zeros((col_n, slice_w - 128), F32)], axis=1)
+    line = iota((col_n, experts), 0)
+    lane = iota((col_n, experts), 1)
+    tail = jnp.zeros((col_n, slice_w - 128), F32)
+    for k in range(2):
+        count = dot_t(bits(lane == 2 * line + k), named.astype(BF))
+        count = jnp.sum(count, axis=1, keepdims=True)
+        tail = jnp.where(iota(tail.shape, 1) == k, count, tail)
+    last = jnp.concatenate([pairs[:, 2 * slice_w :], tail], axis=1)
     data = jnp.concatenate(
         [mine, pairs[:, :slice_w].astype(BF), pairs[:, slice_w : 2 * slice_w].astype(BF), last.astype(BF)],
         axis=0,
@@ -197,25 +206,45 @@
     decw_ref[...] = dot(even, dec.astype(BF))
 
 
-def head_kernel(got_ref, val_ref, proj_ref, res_ref, send_ref):
+def head_kernel(got_ref, val_ref, proj_ref, res_ref, send_ref, keep_ref, info_ref):
     r = lax.axis_index("req")
     b = lax.axis_index("blk")
     n_src, block, slice_w = got_ref.shape
     n_dst, n_out, _ = send_ref.shape
-    n_slot = n_out - 8
-    half = n_slot // 2
-    got = got_ref[...].reshape(n_src * block, slice_w)
-    column, place, second, slot = slot_of(iota((n_slot, n_src * block), 1))
-    target = second * half + column * CAP + slot
-    keep = jnp.logical_and(iota((n_slot, n_src * block), 0) == target, place < 2 * CAP)
-    slots = dot(bits(keep), got).astype(BF)
-    for d in range(n_dst):
-        send_ref[d, :n_slot, :] = slots
-
+    n_slot = n_out - HEAD
+    n_col = n_src * block
+    got = got_ref[...].reshape(n_col, slice_w)
     line = iota((3 * n_src, n_src * block), 0)
     part = iota((3 * n_src, n_src * block), 1) == (line & (n_src - 1)) * block + 12 + (line >> 5)
     part = dot(bits(part), got)
     stats = part[2 * n_src :]
+
+    count = stats[:, 128:]
+    earlier = bits(iota((n_src, n_src), 1) < iota((n_src, n_src), 0))
+    before = dot(earlier, count.astype(BF))
+    spread = bits(iota((n_src, n_col), 1) >> 4 == iota((n_src, n_col), 0))
+    table = jnp.concatenate([before, count], axis=1).astype(BF)
+    table = lax.dot_general(table, spread, (((0,), (0,)), ((), ())), preferred_element_type=F32)
+    used = jnp.sum(count, axis=0, keepdims=True)
+    first_n = used[:, 0:1]
+    column, place, second, slot = slot_of(iota((1, n_col), 1))
+    slot = slot.astype(F32)
+    width = count.shape[1]
+    target = jnp.where(second == 1, table[1:2] + first_n, table[0:1]) + slot
+    named = jnp.where(second == 1, table[width + 1 : width + 2], table[width : width + 1])
+    target = jnp.where(jnp.logical_and(slot < named, place < 2 * CAP), target, -1.0)
+    keep = bits(iota((n_slot, n_col), 0).astype(F32) == target)
+    keep_ref[...] = keep
+    slots = dot(keep, got).astype(BF)
+    for d in range(n_dst):
+        send_ref[d, HEAD:, :] = slots
+    both = first_n + used[:, 1:2]
+    index = jnp.zeros((1, 1), F32)
+    for size in bucket_sizes(n_slot)[:-1]:
+        index = index + jnp.where(both > size, 1.0, 0.0)
+    lane = iota(info_ref.shape, 1)
+    info_ref[...] = jnp.where(lane == 0, index, jnp.where(lane == 1, first_n, 0.0)).astype(I32)
+
     peak = stats[:, 0:1] + stats[:, 1:2] + stats[:, 2:3]
     total = stats[:, 3:4] + stats[:, 4:5] + stats[:, 5:6]
     share = total * jnp.exp(peak - jnp.max(peak, axis=0, keepdims=True))
@@ -234,17 +263,18 @@
     projected = projected + jnp.where(owner, resid, 0.0)
     folded = jnp.concatenate(
         [projected[:, slice_w * j : slice_w * (j + 1)] for j in range(8)], axis=0
-    ).astype(BF)
+    )
+    folded = jnp.concatenate([folded, jnp.zeros((HEAD - 8, slice_w), F32)], axis=0).astype(BF)
     for d in range(n_dst):
-        send_ref[d, n_slot:, :] = folded
+        send_ref[d, :HEAD, :] = folded
 
 
 def sum_kernel(got_ref, send_ref):
-    n_src, n_all, _ = got_ref.shape
-    total = got_ref[0, n_all - 8 :, :].astype(F32)
+    n_src = got_ref.shape[0]
+    total = got_ref[0, :HEAD, :].astype(F32)
     for s in range(1, n_src):
-        total = total + got_ref[s, n_all - 8 :, :].astype(F32)
-    total = total.astype(BF)
+        total = total + got_ref[s, :HEAD, :].astype(F32)
+    total = total[:8].astype(BF)
     for d in range(send_ref.shape[0]):
         send_ref[d] = total
 
@@ -255,16 +285,28 @@
     cols_ref,
     gain_ref,
     decw_ref,
+    info_ref,
     gate_ref,
+    up_hbm,
+    down_hbm,
+    sg_hbm,
+    su_hbm,
+    sd_hbm,
+    out_ref,
+    shared_ref,
+    hid_ref,
     up_ref,
     down_ref,
     sg_ref,
     su_ref,
     sd_ref,
-    out_ref,
-    shared_ref,
-    hid_ref,
+    sems,
 ):
+    loads = []
+    pairs = [(h.at[k], v.at[k]) for k in range(2) for h, v in ((up_hbm, up_ref), (down_hbm, down_ref))]
+    for source, held in pairs + [(sg_hbm, sg_ref), (su_hbm, su_ref), (sd_hbm, sd_ref)]:
+        loads.append(pltpu.make_async_copy(source, held, sems.at[len(loads)]))
+        loads[-1].start()
     b = lax.axis_index("blk")
     n_src, fold, slice_w = got_ref.shape
     dec_n = n_src // 2
@@ -283,47 +325,58 @@
         for j, c in enumerate(chunks)
     ]
 
-    col_n = cols_ref.shape[0]
-    x = jnp.concatenate([cols_ref[...], jnp.concatenate(normed, axis=1)], axis=0)
-    act = silu_mul(dot_t(x, sg_ref[...]), dot_t(x, su_ref[...]))
-    shared = dot(act, sd_ref[...])
-    shared_ref[...] = shared[:col_n].astype(BF)
-    mine = jnp.where(iota((dec_n, 1), 0) == (b >> 1), 1.0, 0.0) * jnp.where((b & 1) == 0, 1.0, 0.0)
-    dec = [mine * shared[col_n:, j * slice_w : (j + 1) * slice_w] for j in range(fold)]
-
     n_dst, n_row, _ = out_ref.shape
-    half = (n_row - 16) // 2
+    half = (n_row - HEAD - SLACK) // 2
+    first_n = jnp.max(jnp.where(iota(info_ref.shape, 1) == 1, info_ref[...], 0).astype(F32)).astype(I32)
+    start = pl.multiple_of(HEAD + ((first_n >> 4) << 4), 16)
+    dec = [jnp.zeros((dec_n, slice_w), F32)] * fold
     for k in range(gate_ref.shape[0]):
-        span = pl.ds(k * half, half)
+        size = half if k == 0 else half + SLACK
+        span = pl.ds(HEAD, size) if k == 0 else pl.ds(start, size)
         gate, up = 0.0, 0.0
+        loads[2 * k].wait()
         for s in range(n_dst):
             x = jnp.concatenate([rows_ref[s, span, :], normed[s]], axis=0)
             lanes = slice(s * slice_w, (s + 1) * slice_w)
             gate = gate + dot_t(x, gate_ref[k, :, lanes])
             up = up + dot_t(x, up_ref[k, :, lanes])
         act = silu_mul(gate, up)
+        loads[2 * k + 1].wait()
+        later = iota((size, slice_w), 0) + (start - HEAD) >= first_n
         for d in range(n_dst):
             out = dot(act, down_ref[k, :, d * slice_w : (d + 1) * slice_w])
-            out_ref[d, span, :] = out[:half].astype(BF)
-            dec[d] = dec[d] + decw_ref[:, k : k + 1] * out[half:]
+            dec[d] = dec[d] + decw_ref[:, k : k + 1] * out[size:]
+            rows = out[:size]
+            if k == 1:
+                rows = jnp.where(later, rows, out_ref[d, span, :].astype(F32))
+            out_ref[d, span, :] = rows.astype(BF)
+
+    col_n = cols_ref.shape[0]
+    for load in loads[4:]:
+        load.wait()
+    x = jnp.concatenate([cols_ref[...], jnp.concatenate(normed, axis=1)], axis=0)
+    act = silu_mul(dot_t(x, sg_ref[...]), dot_t(x, su_ref[...]))
+    shared = dot(act, sd_ref[...])
+    shared_ref[...] = shared[:col_n].astype(BF)
+    mine = jnp.where(iota((dec_n, 1), 0) == (b >> 1), 1.0, 0.0) * jnp.where((b & 1) == 0, 1.0, 0.0)
+    dec = [dec[j] + mine * shared[col_n:, j * slice_w : (j + 1) * slice_w] for j in range(fold)]
 
     line = iota((n_line, n_line), 0)
     col = iota((n_line, n_line), 1)
     swap = bits(col == (line & 7) * dec_n + (line >> 3))
     turned = dot(swap, jnp.concatenate([d.astype(BF) for d in dec], axis=0)).astype(BF)
-    out_ref[:, n_row - 16 :, :] = turned.reshape(n_dst, 16, slice_w)
+    out_ref[:, :HEAD, :] = turned.reshape(n_dst, 16, slice_w)
     hid_ref[...] = dot(swap, hidden).reshape(hid_ref.shape).astype(BF)
 
 
 def hidden_sum_kernel(got_ref, slots_ref, keep_ref, give_ref):
     b = lax.axis_index("blk")
     n_src = got_ref.shape[0]
-    n_slot = slots_ref.shape[0]
     total = got_ref[0].astype(F32)
     for s in range(1, n_src):
         total = total + got_ref[s].astype(F32)
-    slots_ref[...] = total[:n_slot].astype(BF)
-    dec = total[n_slot:]
+    slots_ref[...] = total[HEAD:].astype(BF)
+    dec = total[:HEAD]
     low = jnp.concatenate([dec[0:4], dec[8:12]], axis=0)
     high = jnp.concatenate([dec[4:8], dec[12:16]], axis=0)
     even = (b & 1) == 0
@@ -331,20 +384,15 @@
     give_ref[...] = jnp.where(even, high, low).astype(BF)
 
 
-def return_kernel(slots_ref, keep_ref, other_ref, send_ref):
-    n_slot = slots_ref.shape[0]
+def return_kernel(slots_ref, keep_ref, mine_ref, other_ref, send_ref):
     n_dst, block, _ = send_ref.shape
-    half = n_slot // 2
-    dec = (keep_ref[...] + other_ref[...].astype(F32)).astype(BF)
-    data = jnp.concatenate([slots_ref[...], dec, jnp.zeros_like(dec)], axis=0)
-    column, place, second, slot = slot_of(iota((n_dst * block, n_slot + 16), 0))
-    col = iota((n_dst * block, n_slot + 16), 1)
-    source = jnp.where(
-        place < 2 * CAP,
-        second * half + column * CAP + slot,
-        n_slot + 4 * (column & 1) + place - 2 * CAP,
-    )
-    send_ref[...] = dot(bits(col == source), data).astype(BF).reshape(send_ref.shape)
+    dec = (mine_ref[...] + other_ref[...].astype(F32)).astype(BF)
+    column, place, second, slot = slot_of(iota((n_dst * block, 16), 0))
+    source = jnp.where(place < 2 * CAP, -1, 4 * (column & 1) + place - 2 * CAP)
+    out = dot(bits(iota((n_dst * block, 16), 1) == source), jnp.concatenate([dec, jnp.zeros_like(dec)], axis=0))
+    back = (((0,), (0,)), ((), ()))
+    out = out + lax.dot_general(keep_ref[...], slots_ref[...], back, preferred_element_type=F32)
+    send_ref[...] = out.astype(BF).reshape(send_ref.shape)
 
 
 def combine_kernel(got_ref, comb_ref, shared_ref, hid_ref, send_ref, dec_ref):
@@ -391,7 +439,11 @@
     ).astype(BF)
 
 
-def call(kernel, outs, args, flops, moved, specs=None, scratch=()):
+def bucket_sizes(n_slot):
+    return tuple(range(n_slot // 2, n_slot + 1, 32))
+
+
+def call(kernel, outs, args, flops, moved, specs=None, scratch=(), room=16 << 20):
     return pl.pallas_call(
         kernel,
         out_shape=outs,
@@ -399,7 +451,7 @@
         out_specs=jax.tree.map(lambda _: VMEM, outs),
         scratch_shapes=scratch,
         cost_estimate=pl.CostEstimate(flops=flops, bytes_accessed=moved, transcendentals=0),
-        compiler_params=pltpu.CompilerParams(vmem_limit_bytes=16 << 20),
+        compiler_params=pltpu.CompilerParams(vmem_limit_bytes=room),
     )(*args)
 
 
@@ -479,44 +531,60 @@
         )
         got = exchange(sent, "blk")
     with jax.named_scope("heads"):
-        sent = call(
+        sent, keep, info = call(
             head_kernel,
-            shape(req_n, n_slot + 8, slice_w),
+            (
+                shape(req_n, n_slot + HEAD, slice_w),
+                shape(n_slot, blk_n * 16),
+                shape(8, 128, dtype=I32),
+            ),
             (got, absorb_value, out_proj, decode_resid),
             10**8,
             3 * 10**6,
         )
-        rows = exchange(sent, "req")
+        index = info[0, 0]
+
+        def by_size(payload, height):
+            def branch(size):
+                def run(rows):
+                    moved = exchange(rows[:, : HEAD + size], "req")
+                    return jnp.pad(moved, ((0, 0), (0, height - HEAD - size), (0, 0)))
+
+                return run
+
+            return lax.switch(index, [branch(size) for size in bucket_sizes(n_slot)], payload)
+
+        rows = by_size(sent, n_slot + HEAD + SLACK)
+        rows = pltpu.with_memory_space_constraint(rows, pltpu.VMEM)
     with jax.named_scope("hidden"):
         sent = call(sum_kernel, shape(blk_n, 8, slice_w), (rows,), 10**5, 3 * 10**5)
         got = exchange(sent, "blk")
     with jax.named_scope("experts"):
+        streamed = [
+            jnp.swapaxes(expert_up, 1, 2),
+            expert_down,
+            shared_gate.T,
+            shared_up.T,
+            shared_down,
+        ]
         sent, shared, hidden = call(
             terms_kernel,
             (
-                shape(req_n, n_slot + 16, slice_w),
+                shape(req_n, n_slot + HEAD + SLACK, slice_w),
                 shape(col_n, width),
                 shape(2 * req_n, 8, slice_w),
             ),
-            (
-                got,
-                rows,
-                cols,
-                gain,
-                decw,
-                jnp.swapaxes(expert_gate, 1, 2),
-                jnp.swapaxes(expert_up, 1, 2),
-                expert_down,
-                shared_gate.T,
-                shared_up.T,
-                shared_down,
-            ),
+            (got, rows, cols, gain, decw, info, jnp.swapaxes(expert_gate, 1, 2))
+            + tuple(pltpu.with_memory_space_constraint(a, pltpu.HBM) for a in streamed),
             8 * 10**9,
             12 * 10**6,
-        )
-        got = exchange(sent, "req")
+            specs=[VMEM] * 7 + [pl.BlockSpec(memory_space=pltpu.HBM)] * 5,
+            scratch=[pltpu.VMEM(a.shape, a.dtype) for a in streamed] + [pltpu.SemaphoreType.DMA((7,))],
+            room=24 << 20,
+        )
+        got = by_size(sent, n_slot + HEAD)
     with jax.named_scope("return"):
-        slots, keep, give = call(
+        slots, mine, give = call(
             hidden_sum_kernel,
             (shape(n_slot, slice_w), shape(8, slice_w, dtype=F32), shape(8, slice_w)),
             (got,),
@@ -524,7 +592,7 @@
             2 * 10**6,
         )
         other = lax.ppermute(give, "blk", sibling)
-        sent = call(return_kernel, shape(blk_n, 16, slice_w), (slots, keep, other), 10**8, 10**6)
+        sent = call(return_kernel, shape(blk_n, 16, slice_w), (slots, keep, mine, other), 10**8, 10**6)
         got = exchange(sent, "blk")
     with jax.named_scope("combine"):
         sent, own_row = call(

time: 142 us -> 136 us (0.958)
  blocking collectives: 118 us -> 109 us
  Pallas kernels: 9.84 us -> 12 us
    all_to_all x6, blocking collectives: 118 us -> 109 us  [exchange(): return lax.all_to_all(payload, axis, 0, 0, tiled=True)]
    pallas_call x9, Pallas kernels: 9.84 us -> 12 us  [call(): pl.pallas_call(kernel, out_shape=outs, in_specs=specs or [VMEM] * len(arg...]
where the time goes in v4:
time: 136 us
  blocking collectives  109 us (80%)
  Pallas kernels  12 us (9%)
  waiting for transfers between devices  8.25 us (6%)
  starting transfers between devices  4.59 us (3%)
  between operations  1.4 us (1%)
    all_to_all x6, blocking collectives, exchange(): return lax.all_to_all(payload, axis, 0, 0, tiled=True)  109 us
    pallas_call x9, Pallas kernels, call(): pl.pallas_call(kernel, out_shape=outs, in_specs=specs or [VMEM] * len(arg...  12 us
    all_to_all x1, waiting for transfers between devices, exchange(): return lax.all_to_all(payload, axis, 0, 0, tiled=True)  5.93 us
    all_to_all x1, starting transfers between devices, exchange(): return lax.all_to_all(payload, axis, 0, 0, tiled=True)  4.5 us
  transfers between devices with their start and end apart: 3, of which 3 were waited for; matrix products, arithmetic and copies ran while one was open for 0% of the time, Pallas kernels for 0%

profile of v4, /device:TPU:2, one launch (start us, length us, event | category | flops | bytes accessed | tf_op | source)
XLA Modules:
  0.0 136.0 jit_solution(8348614819754083519)
XLA Ops:
  0.6 0.0 copy-start
  0.6 0.0 copy-start.1
  0.7 0.0 copy-start.3
  0.7 3.1 %start.1 = bf16[8,4,2816]{2,1,0:T(4,128)(2,1)S(1)} custom-call(bf16[2,16,192]{2,1,0:T(8,128)(2,1)} %refs_0_.1, bf16[16,128,512]{2,1,0:T(8,128)(2,1)} %refs_1_.1, bf16[4,2048]{1,0:T(4,128)(2,1)} %res_ref.3, f32[1,2048]{1,0:T(1,128)} %bitcast.7, s32[4,6]{1,0:T(4,128)} %refs_4_.1, f32[4,6]{1,0:T(4,128)} %refs_5_.1, s32[2,6]{1,0:T(2,128)} %refs_6_.1, ...), custom_call_target="tpu_custom_call" | custom-call | flops 100000000 | bytes 4000000 | tf_op jit(solution)/shard_map/start/pallas_call | solution.py:447
  3.8 14.4 %all_to_all.95.got_ref = bf16[8,4,2816]{2,1,0:T(4,128)(2,1)S(1)} all-to-all(bf16[8,4,2816]{2,1,0:T(4,128)(2,1)S(1)} %start.1), channel_id=1, replica_groups=mesh['req'=8,'blk'=32] {'req'}, dimensions={0} | all-to-all | bytes 360448 | tf_op jit(solution)/shard_map/start/all_to_all | solution.py:21
  18.2 0.9 route.1
  19.1 21.9 %all_to_all.96.got_ref = bf16[32,16,256]{2,1,0:T(8,128)(2,1)S(1)} all-to-all(bf16[32,16,256]{2,1,0:T(8,128)(2,1)S(1)} %get-tuple-element.47), channel_id=1, replica_groups=mesh['req'=8,'blk'=32] {'blk'}, dimensions={0} | all-to-all | bytes 524288 | tf_op jit(solution)/shard_map/route/all_to_all | solution.py:21
  41.1 0.0 copy-done
  41.1 0.0 copy-done.1
  41.1 0.0 copy-done.3
  41.1 1.0 heads.1
  42.1 0.5 slice.42
  43.2 17.6 %conditional.2 = (bf16[8,448,256]{2,1,0:T(8,128)(2,1)S(1)}) conditional(s32[]{:T(128)} %bitcast.2, bf16[8,400,256]{2,1,0:T(8,128)(2,1)S(1)} %get-tuple-element.49, bf16[8,400,256]{2,1,0:T(8,128)(2,1)S(1)} %get-tuple-element.49, bf16[8,400,256]{2,1,0:T(8,128)(2,1)S(1)} %get-tuple-element.49, ...), branch_computations={%region_0.1_spmd, %region_1.2_spmd, %region_2.3_spmd, %region_3.4_... | conditional | bytes 9371658 | solution.py:555
  43.2 0.1 slice.28
  43.3 17.4 %all_to_all.81 = bf16[8,208,256]{2,1,0:T(8,128)(2,1)S(1)} all-to-all(bf16[8,208,256]{2,1,0:T(8,128)(2,1)S(1)} %slice.28), channel_id=1, replica_groups=mesh['req'=8,'blk'=32] {'req'}, dimensions={0} | all-to-all | bytes 1703936 | tf_op jit(solution)/shard_map/heads/cond/branch_0_fun/all_to_all | solution.py:21
  60.7 0.1 pad.39
  60.9 0.0 copy-start.4
  60.9 0.0 copy-start.5
  60.9 17.5 %all_to_all.97.got_ref = bf16[32,8,256]{2,1,0:T(8,128)(2,1)S(1)} all-to-all(bf16[32,8,256]{2,1,0:T(8,128)(2,1)S(1)} %hidden.1), channel_id=1, replica_groups=mesh['req'=8,'blk'=32] {'blk'}, dimensions={0} | all-to-all | bytes 262144 | tf_op jit(solution)/shard_map/hidden/all_to_all | solution.py:21
  78.4 0.0 copy-done.4
  78.4 0.0 copy-done.5
  78.4 4.8 %experts.1 = (bf16[8,448,256]{2,1,0:T(8,128)(2,1)S(1)}, bf16[32,2048]{1,0:T(8,128)(2,1)S(1)}, bf16[16,8,256]{2,1,0:T(8,128)(2,1)S(1)}) custom-call(bf16[32,8,256]{2,1,0:T(8,128)(2,1)S(1)} %all_to_all.97.got_ref, bf16[8,448,256]{2,1,0:T(8,128)(2,1)S(1)} %get-tuple-element.62.got_ref.rows_ref, bf16[32,2048]{1,0:T(8,128)(2,1)S(1)} %get-tuple-element.50.cols_ref, ...), custom_call_target="tpu_custom_call" | custom-call | flops 8000000000 | bytes 12000000 | tf_op jit(solution)/shard_map/experts/pallas_call | solution.py:447
  83.2 17.5 %conditional.3 = (bf16[8,400,256]{2,1,0:T(8,128)(2,1)S(1)}) conditional(s32[]{:T(128)} %bitcast.2, bf16[8,448,256]{2,1,0:T(8,128)(2,1)S(1)} %get-tuple-element.52, bf16[8,448,256]{2,1,0:T(8,128)(2,1)S(1)} %get-tuple-element.52, bf16[8,448,256]{2,1,0:T(8,128)(2,1)S(1)} %get-tuple-element.52, ...), branch_computations={%region_7.8_spmd, %region_8.9_spmd, %region_9.10_spmd, %region_10.... | conditional | bytes 9175050 | solution.py:555
  83.3 0.1 slice.34
  83.3 17.3 %all_to_all.88 = bf16[8,208,256]{2,1,0:T(8,128)(2,1)S(1)} all-to-all(bf16[8,208,256]{2,1,0:T(8,128)(2,1)S(1)} %slice.34), channel_id=1, replica_groups=mesh['req'=8,'blk'=32] {'req'}, dimensions={0} | all-to-all | bytes 1703936 | tf_op jit(solution)/shard_map/experts/cond/branch_0_fun/all_to_all | solution.py:21
  100.6 0.1 pad.46
  100.7 0.2 return.2
  100.9 0.0 copy-start.2
  101.0 0.1 collective-permute-start
  101.1 1.2 collective-permute-done.other_ref
  102.2 0.4 return.3
  102.6 20.2 %all_to_all.98.got_ref = bf16[32,16,256]{2,1,0:T(8,128)(2,1)S(1)} all-to-all(bf16[32,16,256]{2,1,0:T(8,128)(2,1)S(1)} %return.3), channel_id=1, replica_groups=mesh['req'=8,'blk'=32] {'blk'}, dimensions={0} | all-to-all | bytes 524288 | tf_op jit(solution)/shard_map/return/all_to_all | solution.py:21
  122.8 0.9 combine.1
  123.7 4.5 %all-to-all-start.18 = ((bf16[8,4,2560]{2,1,0:T(4,128)(2,1)}), bf16[8,4,2560]{2,1,0:T(4,128)(2,1)S(1)}, u32[]{:S(2)}, u32[]{:S(2)}) async-start(bf16[8,4,2560]{2,1,0:T(4,128)(2,1)} %get-tuple-element.60), calls=%async_computation.18 | async-start | bytes 327680 | tf_op jit(solution)/shard_map/combine/all_to_all | solution.py:21
  128.2 0.0 collective-permute-start.1
  128.2 1.2 collective-permute-done.1.other_ref
  129.4 5.9 %all-to-all-done.18.got_ref = bf16[8,4,2560]{2,1,0:T(4,128)(2,1)S(1)} async-done(((bf16[8,4,2560]{2,1,0:T(4,128)(2,1)}), bf16[8,4,2560]{2,1,0:T(4,128)(2,1)S(1)}, u32[]{:S(2)}, u32[]{:S(2)}) %all-to-all-start.18) | async-done | bytes 163872 | tf_op jit(solution)/shard_map/combine/all_to_all | solution.py:21
  135.3 0.0 copy-done.2
  135.3 0.7 finish.1
  (1 shorter events, 0.0 us)
Async XLA Ops:
  0.6 40.4 %copy-start = (bf16[2,128,2048]{2,1,0:T(8,128)(2,1)S(1)}, bf16[2,128,2048]{2,1,0:T(8,128)(2,1)}, u32[]{:S(2)}) copy-start(bf16[2,128,2048]{2,1,0:T(8,128)(2,1)} %proj_ref.1) | copy-start | bytes 3145732
  0.6 40.4 %copy-start.1 = (bf16[2,512,128]{2,1,0:T(8,128)(2,1)S(1)}, bf16[2,512,128]{2,1,0:T(8,128)(2,1)}, u32[]{:S(2)}) copy-start(bf16[2,512,128]{2,1,0:T(8,128)(2,1)} %val_ref.1) | copy-start | bytes 786436
  0.7 40.4 %copy-start.3 = (bf16[2,2048]{1,0:T(2,128)(2,1)S(1)}, bf16[2,2048]{1,0:T(2,128)(2,1)}, u32[]{:S(2)}) copy-start(bf16[2,2048]{1,0:T(2,128)(2,1)} %res_ref.2) | copy-start | bytes 24580
  60.9 17.5 %copy-start.4 = (f32[2048]{0:T(1024)S(1)}, f32[2048]{0:T(1024)}, u32[]{:S(2)}) copy-start(f32[2048]{0:T(1024)} %param.44) | copy-start | bytes 24580
  60.9 17.5 %copy-start.5 = (bf16[2,2048,176]{1,2,0:T(8,128)(2,1)S(1)}, bf16[2,2048,176]{1,2,0:T(8,128)(2,1)}, u32[]{:S(2)}) copy-start(bf16[2,2048,176]{1,2,0:T(8,128)(2,1)} %param.48) | copy-start | bytes 4325380
  100.9 34.4 %copy-start.2 = (bf16[4,2048]{1,0:T(4,128)(2,1)S(1)}, bf16[4,2048]{1,0:T(4,128)(2,1)}, u32[]{:S(2)}) copy-start(bf16[4,2048]{1,0:T(4,128)(2,1)} %res_ref.3) | copy-start | bytes 49156
  101.0 1.3 collective-permute-start
  123.7 11.6 %all-to-all-start.18 = ((bf16[8,4,2560]{2,1,0:T(4,128)(2,1)}), bf16[8,4,2560]{2,1,0:T(4,128)(2,1)S(1)}, u32[]{:S(2)}, u32[]{:S(2)}) async-start(bf16[8,4,2560]{2,1,0:T(4,128)(2,1)} %get-tuple-element.60), calls=%async_computation.18 | async-start | bytes 327680 | tf_op jit(solution)/shard_map/combine/all_to_all | solution.py:21
  128.2 1.2 collective-permute-start.1

commit v5 on v4

--- a/solution.py
+++ b/solution.py
@@ -287,26 +287,15 @@
     decw_ref,
     info_ref,
     gate_ref,
-    up_hbm,
-    down_hbm,
-    sg_hbm,
-    su_hbm,
-    sd_hbm,
-    out_ref,
-    shared_ref,
-    hid_ref,
     up_ref,
     down_ref,
     sg_ref,
     su_ref,
     sd_ref,
-    sems,
+    out_ref,
+    shared_ref,
+    hid_ref,
 ):
-    loads = []
-    pairs = [(h.at[k], v.at[k]) for k in range(2) for h, v in ((up_hbm, up_ref), (down_hbm, down_ref))]
-    for source, held in pairs + [(sg_hbm, sg_ref), (su_hbm, su_ref), (sd_hbm, sd_ref)]:
-        loads.append(pltpu.make_async_copy(source, held, sems.at[len(loads)]))
-        loads[-1].start()
     b = lax.axis_index("blk")
     n_src, fold, slice_w = got_ref.shape
     dec_n = n_src // 2
@@ -325,23 +314,28 @@
         for j, c in enumerate(chunks)
     ]
 
+    col_n = cols_ref.shape[0]
+    x = jnp.concatenate([cols_ref[...], jnp.concatenate(normed, axis=1)], axis=0)
+    act = silu_mul(dot_t(x, sg_ref[...]), dot_t(x, su_ref[...]))
+    shared = dot(act, sd_ref[...])
+    shared_ref[...] = shared[:col_n].astype(BF)
+    mine = jnp.where(iota((dec_n, 1), 0) == (b >> 1), 1.0, 0.0) * jnp.where((b & 1) == 0, 1.0, 0.0)
+    dec = [mine * shared[col_n:, j * slice_w : (j + 1) * slice_w] for j in range(fold)]
+
     n_dst, n_row, _ = out_ref.shape
     half = (n_row - HEAD - SLACK) // 2
     first_n = jnp.max(jnp.where(iota(info_ref.shape, 1) == 1, info_ref[...], 0).astype(F32)).astype(I32)
     start = pl.multiple_of(HEAD + ((first_n >> 4) << 4), 16)
-    dec = [jnp.zeros((dec_n, slice_w), F32)] * fold
     for k in range(gate_ref.shape[0]):
         size = half if k == 0 else half + SLACK
         span = pl.ds(HEAD, size) if k == 0 else pl.ds(start, size)
         gate, up = 0.0, 0.0
-        loads[2 * k].wait()
         for s in range(n_dst):
             x = jnp.concatenate([rows_ref[s, span, :], normed[s]], axis=0)
             lanes = slice(s * slice_w, (s + 1) * slice_w)
             gate = gate + dot_t(x, gate_ref[k, :, lanes])
             up = up + dot_t(x, up_ref[k, :, lanes])
         act = silu_mul(gate, up)
-        loads[2 * k + 1].wait()
         later = iota((size, slice_w), 0) + (start - HEAD) >= first_n
         for d in range(n_dst):
             out = dot(act, down_ref[k, :, d * slice_w : (d + 1) * slice_w])
@@ -350,16 +344,6 @@
             if k == 1:
                 rows = jnp.where(later, rows, out_ref[d, span, :].astype(F32))
             out_ref[d, span, :] = rows.astype(BF)
-
-    col_n = cols_ref.shape[0]
-    for load in loads[4:]:
-        load.wait()
-    x = jnp.concatenate([cols_ref[...], jnp.concatenate(normed, axis=1)], axis=0)
-    act = silu_mul(dot_t(x, sg_ref[...]), dot_t(x, su_ref[...]))
-    shared = dot(act, sd_ref[...])
-    shared_ref[...] = shared[:col_n].astype(BF)
-    mine = jnp.where(iota((dec_n, 1), 0) == (b >> 1), 1.0, 0.0) * jnp.where((b & 1) == 0, 1.0, 0.0)
-    dec = [dec[j] + mine * shared[col_n:, j * slice_w : (j + 1) * slice_w] for j in range(fold)]
 
     line = iota((n_line, n_line), 0)
     col = iota((n_line, n_line), 1)
@@ -443,7 +427,7 @@
     return tuple(range(n_slot // 2, n_slot + 1, 32))
 
 
-def call(kernel, outs, args, flops, moved, specs=None, scratch=(), room=16 << 20):
+def call(kernel, outs, args, flops, moved, specs=None, scratch=()):
     return pl.pallas_call(
         kernel,
         out_shape=outs,
@@ -451,7 +435,7 @@
         out_specs=jax.tree.map(lambda _: VMEM, outs),
         scratch_shapes=scratch,
         cost_estimate=pl.CostEstimate(flops=flops, bytes_accessed=moved, transcendentals=0),
-        compiler_params=pltpu.CompilerParams(vmem_limit_bytes=room),
+        compiler_params=pltpu.CompilerParams(vmem_limit_bytes=16 << 20),
     )(*args)
 
 
@@ -557,16 +541,9 @@
         rows = by_size(sent, n_slot + HEAD + SLACK)
         rows = pltpu.with_memory_space_constraint(rows, pltpu.VMEM)
     with jax.named_scope("hidden"):
-        sent = call(sum_kernel, shape(blk_n, 8, slice_w), (rows,), 10**5, 3 * 10**5)
+        sent = call(sum_kernel, shape(blk_n, 8, slice_w), (rows,), 10**10, 5 * 10**7)
         got = exchange(sent, "blk")
     with jax.named_scope("experts"):
-        streamed = [
-            jnp.swapaxes(expert_up, 1, 2),
-            expert_down,
-            shared_gate.T,
-            shared_up.T,
-            shared_down,
-        ]
         sent, shared, hidden = call(
             terms_kernel,
             (
@@ -574,13 +551,22 @@
                 shape(col_n, width),
                 shape(2 * req_n, 8, slice_w),
             ),
-            (got, rows, cols, gain, decw, info, jnp.swapaxes(expert_gate, 1, 2))
-            + tuple(pltpu.with_memory_space_constraint(a, pltpu.HBM) for a in streamed),
+            (
+                got,
+                rows,
+                cols,
+                gain,
+                decw,
+                info,
+                jnp.swapaxes(expert_gate, 1, 2),
+                jnp.swapaxes(expert_up, 1, 2),
+                expert_down,
+                shared_gate.T,
+                shared_up.T,
+                shared_down,
+            ),
             8 * 10**9,
             12 * 10**6,
-            specs=[VMEM] * 7 + [pl.BlockSpec(memory_space=pltpu.HBM)] * 5,
-            scratch=[pltpu.VMEM(a.shape, a.dtype) for a in streamed] + [pltpu.SemaphoreType.DMA((7,))],
-            room=24 << 20,
         )
         got = by_size(sent, n_slot + HEAD)
     with jax.named_scope("return"):

time: 136 us -> 133 us (0.978)
  Pallas kernels: 12 us -> 10.5 us
    pallas_call x9, Pallas kernels: 12 us -> 10.5 us  [call(): pl.pallas_call(kernel, out_shape=outs, in_specs=specs or [VMEM] * len(arg...]
where the time goes in v5:
time: 133 us; the launch traced here: 134 us
  blocking collectives  108 us (81%)
  Pallas kernels  10.5 us (8%)
  waiting for transfers between devices  8.28 us (6%)
  starting transfers between devices  4.55 us (3%)
  between operations  1.48 us (1%)
    all_to_all x6, blocking collectives, exchange(): return lax.all_to_all(payload, axis, 0, 0, tiled=True)  108 us
    pallas_call x9, Pallas kernels, call(): pl.pallas_call(kernel, out_shape=outs, in_specs=specs or [VMEM] * len(arg...  10.5 us
    all_to_all x1, waiting for transfers between devices, exchange(): return lax.all_to_all(payload, axis, 0, 0, tiled=True)  5.97 us
    all_to_all x1, starting transfers between devices, exchange(): return lax.all_to_all(payload, axis, 0, 0, tiled=True)  4.46 us
  transfers between devices with their start and end apart: 3, of which 3 were waited for; matrix products, arithmetic and copies ran while one was open for 0% of the time, Pallas kernels for 0%

profile of v5, /device:TPU:2, one launch (start us, length us, event | category | flops | bytes accessed | tf_op | source)
XLA Modules:
  0.0 133.7 jit_solution(10649308104826483962)
XLA Ops:
  0.6 0.0 copy-start
  0.6 0.0 copy-start.1
  0.7 0.0 copy-start.3
  0.7 3.1 %start.1 = bf16[8,4,2816]{2,1,0:T(4,128)(2,1)S(1)} custom-call(bf16[2,16,192]{2,1,0:T(8,128)(2,1)} %refs_0_.1, bf16[16,128,512]{2,1,0:T(8,128)(2,1)} %refs_1_.1, bf16[4,2048]{1,0:T(4,128)(2,1)} %res_ref.3, f32[1,2048]{1,0:T(1,128)} %bitcast.7, s32[4,6]{1,0:T(4,128)} %refs_4_.1, f32[4,6]{1,0:T(4,128)} %refs_5_.1, s32[2,6]{1,0:T(2,128)} %refs_6_.1, ...), custom_call_target="tpu_custom_call" | custom-call | flops 100000000 | bytes 4000000 | tf_op jit(solution)/shard_map/start/pallas_call | solution.py:431
  3.8 14.4 %all_to_all.95.got_ref = bf16[8,4,2816]{2,1,0:T(4,128)(2,1)S(1)} all-to-all(bf16[8,4,2816]{2,1,0:T(4,128)(2,1)S(1)} %start.1), channel_id=1, replica_groups=mesh['req'=8,'blk'=32] {'req'}, dimensions={0} | all-to-all | bytes 360448 | tf_op jit(solution)/shard_map/start/all_to_all | solution.py:21
  18.2 0.9 route.1
  19.1 21.9 %all_to_all.96.got_ref = bf16[32,16,256]{2,1,0:T(8,128)(2,1)S(1)} all-to-all(bf16[32,16,256]{2,1,0:T(8,128)(2,1)S(1)} %get-tuple-element.47), channel_id=1, replica_groups=mesh['req'=8,'blk'=32] {'blk'}, dimensions={0} | all-to-all | bytes 524288 | tf_op jit(solution)/shard_map/route/all_to_all | solution.py:21
  41.1 0.0 copy-done
  41.1 0.0 copy-done.1
  41.1 0.0 copy-done.3
  41.1 1.0 heads.1
  42.1 0.5 slice.42
  43.2 21.2 %conditional.2 = (bf16[8,448,256]{2,1,0:T(8,128)(2,1)S(1)}) conditional(s32[]{:T(128)} %bitcast.2, bf16[8,400,256]{2,1,0:T(8,128)(2,1)S(1)} %get-tuple-element.49, bf16[8,400,256]{2,1,0:T(8,128)(2,1)S(1)} %get-tuple-element.49, bf16[8,400,256]{2,1,0:T(8,128)(2,1)S(1)} %get-tuple-element.49, ...), branch_computations={%region_0.1_spmd, %region_1.2_spmd, %region_2.3_spmd, %region_3.4_... | conditional | bytes 9371658 | solution.py:539
  43.3 0.1 slice.29
  43.3 21.0 %all_to_all.82 = bf16[8,240,256]{2,1,0:T(8,128)(2,1)S(1)} all-to-all(bf16[8,240,256]{2,1,0:T(8,128)(2,1)S(1)} %slice.29), channel_id=1, replica_groups=mesh['req'=8,'blk'=32] {'req'}, dimensions={0} | all-to-all | bytes 1966080 | tf_op jit(solution)/shard_map/heads/cond/branch_1_fun/all_to_all | solution.py:21
  64.3 0.1 pad.40
  64.4 0.0 copy-start.4
  64.4 0.0 copy-start.5
  64.5 0.0 copy-start.6
  64.5 0.0 copy-start.7
  64.5 0.0 copy-start.8
  64.5 0.0 copy-start.9
  64.5 0.0 copy-start.10
  64.5 13.9 %all_to_all.97.got_ref = bf16[32,8,256]{2,1,0:T(8,128)(2,1)S(1)} all-to-all(bf16[32,8,256]{2,1,0:T(8,128)(2,1)S(1)} %hidden.1), channel_id=1, replica_groups=mesh['req'=8,'blk'=32] {'blk'}, dimensions={0} | all-to-all | bytes 262144 | tf_op jit(solution)/shard_map/hidden/all_to_all | solution.py:21
  78.5 0.0 copy-done.4
  78.5 0.0 copy-done.5
  78.5 0.0 copy-done.6
  78.5 0.0 copy-done.7
  78.5 0.0 copy-done.8
  78.5 0.0 copy-done.9
  78.5 0.0 copy-done.10
  78.5 3.3 %experts.1 = (bf16[8,448,256]{2,1,0:T(8,128)(2,1)S(1)}, bf16[32,2048]{1,0:T(8,128)(2,1)S(1)}, bf16[16,8,256]{2,1,0:T(8,128)(2,1)S(1)}) custom-call(bf16[32,8,256]{2,1,0:T(8,128)(2,1)S(1)} %all_to_all.97.got_ref, bf16[8,448,256]{2,1,0:T(8,128)(2,1)S(1)} %get-tuple-element.62.got_ref.rows_ref, bf16[32,2048]{1,0:T(8,128)(2,1)S(1)} %get-tuple-element.50.cols_ref, ...), custom_call_target="tpu_custom_call" | custom-call | flops 8000000000 | bytes 12000000 | tf_op jit(solution)/shard_map/experts/pallas_call | solution.py:431
  81.9 20.6 %conditional.3 = (bf16[8,400,256]{2,1,0:T(8,128)(2,1)S(1)}) conditional(s32[]{:T(128)} %bitcast.2, bf16[8,448,256]{2,1,0:T(8,128)(2,1)S(1)} %get-tuple-element.52, bf16[8,448,256]{2,1,0:T(8,128)(2,1)S(1)} %get-tuple-element.52, bf16[8,448,256]{2,1,0:T(8,128)(2,1)S(1)} %get-tuple-element.52, ...), branch_computations={%region_7.8_spmd, %region_8.9_spmd, %region_9.10_spmd, %region_10.... | conditional | bytes 9175050 | solution.py:539
  81.9 0.1 slice.35
  82.0 20.4 %all_to_all.89 = bf16[8,240,256]{2,1,0:T(8,128)(2,1)S(1)} all-to-all(bf16[8,240,256]{2,1,0:T(8,128)(2,1)S(1)} %slice.35), channel_id=1, replica_groups=mesh['req'=8,'blk'=32] {'req'}, dimensions={0} | all-to-all | bytes 1966080 | tf_op jit(solution)/shard_map/experts/cond/branch_1_fun/all_to_all | solution.py:21
  102.4 0.1 pad.47
  102.5 0.2 return.2
  102.7 0.0 copy-start.2
  102.7 0.1 collective-permute-start
  102.8 1.2 collective-permute-done.other_ref
  104.0 0.4 return.3
  104.4 16.2 %all_to_all.98.got_ref = bf16[32,16,256]{2,1,0:T(8,128)(2,1)S(1)} all-to-all(bf16[32,16,256]{2,1,0:T(8,128)(2,1)S(1)} %return.3), channel_id=1, replica_groups=mesh['req'=8,'blk'=32] {'blk'}, dimensions={0} | all-to-all | bytes 524288 | tf_op jit(solution)/shard_map/return/all_to_all | solution.py:21
  120.5 0.9 combine.1
  121.4 4.5 %all-to-all-start.18 = ((bf16[8,4,2560]{2,1,0:T(4,128)(2,1)}), bf16[8,4,2560]{2,1,0:T(4,128)(2,1)S(1)}, u32[]{:S(2)}, u32[]{:S(2)}) async-start(bf16[8,4,2560]{2,1,0:T(4,128)(2,1)} %get-tuple-element.60), calls=%async_computation.18 | async-start | bytes 327680 | tf_op jit(solution)/shard_map/combine/all_to_all | solution.py:21
  125.9 0.0 collective-permute-start.1
  125.9 1.2 collective-permute-done.1.other_ref
  127.0 6.0 %all-to-all-done.18.got_ref = bf16[8,4,2560]{2,1,0:T(4,128)(2,1)S(1)} async-done(((bf16[8,4,2560]{2,1,0:T(4,128)(2,1)}), bf16[8,4,2560]{2,1,0:T(4,128)(2,1)S(1)}, u32[]{:S(2)}, u32[]{:S(2)}) %all-to-all-start.18) | async-done | bytes 163872 | tf_op jit(solution)/shard_map/combine/all_to_all | solution.py:21
  133.0 0.0 copy-done.2
  133.0 0.7 finish.1
  (1 shorter events, 0.0 us)
Async XLA Ops:
  0.6 40.4 %copy-start = (bf16[2,128,2048]{2,1,0:T(8,128)(2,1)S(1)}, bf16[2,128,2048]{2,1,0:T(8,128)(2,1)}, u32[]{:S(2)}) copy-start(bf16[2,128,2048]{2,1,0:T(8,128)(2,1)} %proj_ref.1) | copy-start | bytes 3145732
  0.6 40.4 %copy-start.1 = (bf16[2,512,128]{2,1,0:T(8,128)(2,1)S(1)}, bf16[2,512,128]{2,1,0:T(8,128)(2,1)}, u32[]{:S(2)}) copy-start(bf16[2,512,128]{2,1,0:T(8,128)(2,1)} %val_ref.1) | copy-start | bytes 786436
  0.7 40.4 %copy-start.3 = (bf16[2,2048]{1,0:T(2,128)(2,1)S(1)}, bf16[2,2048]{1,0:T(2,128)(2,1)}, u32[]{:S(2)}) copy-start(bf16[2,2048]{1,0:T(2,128)(2,1)} %res_ref.2) | copy-start | bytes 24580
  64.4 14.1 %copy-start.4 = (f32[2048]{0:T(1024)S(1)}, f32[2048]{0:T(1024)}, u32[]{:S(2)}) copy-start(f32[2048]{0:T(1024)} %param.44) | copy-start | bytes 24580
  64.4 14.1 %copy-start.5 = (bf16[2,2048,176]{1,2,0:T(8,128)(2,1)S(1)}, bf16[2,2048,176]{1,2,0:T(8,128)(2,1)}, u32[]{:S(2)}) copy-start(bf16[2,2048,176]{1,2,0:T(8,128)(2,1)} %param.48) | copy-start | bytes 4325380
  64.5 14.0 %copy-start.6 = (bf16[2,2048,176]{1,2,0:T(8,128)(2,1)S(1)}, bf16[2,2048,176]{1,2,0:T(8,128)(2,1)}, u32[]{:S(2)}) copy-start(bf16[2,2048,176]{1,2,0:T(8,128)(2,1)} %param.49) | copy-start | bytes 4325380
  64.5 14.0 %copy-start.7 = (bf16[2,176,2048]{2,1,0:T(8,128)(2,1)S(1)}, bf16[2,176,2048]{2,1,0:T(8,128)(2,1)}, u32[]{:S(2)}) copy-start(bf16[2,176,2048]{2,1,0:T(8,128)(2,1)} %down_ref.1) | copy-start | bytes 4325380
  64.5 14.0 %copy-start.8 = (bf16[2048,352]{0,1:T(8,128)(2,1)S(1)}, bf16[2048,352]{0,1:T(8,128)(2,1)}, u32[]{:S(2)}) copy-start(bf16[2048,352]{0,1:T(8,128)(2,1)} %param.51) | copy-start | bytes 4325380
  64.5 14.0 %copy-start.9 = (bf16[2048,352]{0,1:T(8,128)(2,1)S(1)}, bf16[2048,352]{0,1:T(8,128)(2,1)}, u32[]{:S(2)}) copy-start(bf16[2048,352]{0,1:T(8,128)(2,1)} %param.52) | copy-start | bytes 4325380
  64.5 14.0 %copy-start.10 = (bf16[352,2048]{1,0:T(8,128)(2,1)S(1)}, bf16[352,2048]{1,0:T(8,128)(2,1)}, u32[]{:S(2)}) copy-start(bf16[352,2048]{1,0:T(8,128)(2,1)} %sd_ref.1) | copy-start | bytes 4325380
  102.7 30.3 %copy-start.2 = (bf16[4,2048]{1,0:T(4,128)(2,1)S(1)}, bf16[4,2048]{1,0:T(4,128)(2,1)}, u32[]{:S(2)}) copy-start(bf16[4,2048]{1,0:T(4,128)(2,1)} %res_ref.3) | copy-start | bytes 49156
  102.7 1.3 collective-permute-start
  121.4 11.6 %all-to-all-start.18 = ((bf16[8,4,2560]{2,1,0:T(4,128)(2,1)}), bf16[8,4,2560]{2,1,0:T(4,128)(2,1)S(1)}, u32[]{:S(2)}, u32[]{:S(2)}) async-start(bf16[8,4,2560]{2,1,0:T(4,128)(2,1)} %get-tuple-element.60), calls=%async_computation.18 | async-start | bytes 327680 | tf_op jit(solution)/shard_map/combine/all_to_all | solution.py:21
  125.9 1.2 collective-permute-start.1
